TPU v7x, 32 devices: a whole 2x2x4 slice. The times are simulated.
32 devices in a mesh: gy: 4 (over x, core), gz: 8 (over z, y).
Axes of the slice: x: 2, y: 2, z: 4, core: 2. Of those that a mesh axis runs over, the one named last changes fastest.
Arguments:
- velocity: float32 [3, 384, 6144], P(None, 'gy', 'gz'), may hold values from -250 to 250
- strain: bfloat16 [6, 384, 6144], P(None, 'gy', 'gz'), may hold values from -250 to 250
- cell_height: float32 [384], P('gy'), may hold values from 0.5 to 2
- stencil_reach: int32 [2, 384], P(None, 'gy'), may hold values from 1 to 8, as said below
Outputs:
- coefficient: float32 [384], P('gy')
Inputs may be any that keep to these rules, and one draw needn't show every extreme that they name: `stencil_reach`: in every draw some plane reaches 8 planes on both sides; stencils are cut at the walls by the steps.
All inputs are finite; a program needn't handle non-finite values.
Results may differ from a plain program's by a relative error of at most 0.0003.
Values sent between devices are 32-bit elements; how exact they have to be, the bound alone decides.
A program may use at most 128 MiB of HBM per device.

v0:
```python
import functools

import jax
import jax.numpy as jnp
from jax import lax
from jax.experimental import pallas as pl
from jax.experimental.pallas import tpu as pltpu
from jax.sharding import PartitionSpec as P

NX = 8
HMAX = 8
LANES = 128
ROWS = 16

LEAD_INDEX = (0, 1, 2, 0, 0, 1)
TAIL_INDEX = (0, 1, 2, 1, 2, 2)
TENSOR_WEIGHTS = (1.0, 1.0, 1.0, 2.0, 2.0, 2.0)
FIELDS = 21
PACKED_AT = (
    [(0, c) for c in range(3)]
    + [(1, 0), (1, 1), (1, 2), (1, 9), (1, 11), (1, 10)]
    + [(0, 3 + c) for c in range(6)]
    + [(1, 3 + c) for c in range(6)]
)
MESH = pl.DeviceIdType.MESH


def strain_rate(t):
    squares = 2.0 * (t[0] * t[0] + t[1] * t[1] + t[2] * t[2])
    return jnp.sqrt(squares + 4.0 * (t[3] * t[3] + t[4] * t[4] + t[5] * t[5]))


def lane_index(rows):
    return lax.broadcasted_iota(jnp.int32, (rows, LANES), 1)


def streamwise4(x):
    position = lane_index(x.shape[0]) % NX
    behind = jnp.where(
        position == 0, pltpu.roll(x, LANES + 1 - NX, 1), pltpu.roll(x, 1, 1)
    )
    ahead = jnp.where(
        position == NX - 1, pltpu.roll(x, NX - 1, 1), pltpu.roll(x, LANES - 1, 1)
    )
    return behind + ahead + (x + x)


def horizontal(window, parted):
    shape = (3 * LANES, 2 * LANES)
    source = lax.broadcasted_iota(jnp.int32, shape, 0)
    target = lax.broadcasted_iota(jnp.int32, shape, 1) + LANES // 2
    cells_apart = jnp.abs(source // NX - target // NX)
    along = (source - target) & (NX - 1)
    span = jnp.where(cells_apart == 0, 2.0, jnp.where(cells_apart == 1, 1.0, 0.0))
    stream = jnp.where(along == 0, 2.0, jnp.where((along == 1) | (along == NX - 1), 1.0, 0.0))
    both = span * stream
    if parted:
        both = jnp.where((source < 2 * LANES) == (target < 2 * LANES), both, 0.0)
    both = both.astype(jnp.bfloat16)
    window[0 : 3 * LANES, :] = both
    window[3 * LANES : 6 * LANES, :] = both


def halves(x):
    high = x.astype(jnp.bfloat16)
    return high, (x - high.astype(jnp.float32)).astype(jnp.bfloat16)


def kernel(
    n_y,
    n_z,
    vel_hbm,
    strain_hbm,
    height_hbm,
    reach_hbm,
    out,
    vel,
    strain,
    height,
    reach,
    pieces,
    wall,
    window,
    window_parted,
    packed_pieces,
    packed_out,
    filt,
    halo_u,
    halo_s,
    send_s,
    strips,
    halo_strips,
    heights,
    halo_heights,
    acc,
    part,
    slots,
    send_sem,
    recv_sem,
    part_send,
    part_recv,
    load_sem,
    inside,
):
    planes, cells = vel.shape[1], vel.shape[2]
    all_planes = planes + 2 * HMAX
    loads = [
        pltpu.make_async_copy(strain_hbm, strain.at[:, 0:planes, :], load_sem.at[0]),
        pltpu.make_async_copy(vel_hbm, vel, load_sem.at[1]),
        pltpu.make_async_copy(height_hbm, height, load_sem.at[2]),
        pltpu.make_async_copy(reach_hbm, reach, load_sem.at[3]),
    ]
    for load in loads:
        load.start()
    tiles = cells // LANES
    my = lax.axis_index("gy")
    mz = lax.axis_index("gz")
    right = lax.rem(mz + 1, n_z)
    left = lax.rem(mz + n_z - 1, n_z)
    has_low = my > 0
    has_high = my < n_y - 1
    low = my - 1
    high = my + 1

    barrier = pltpu.get_barrier_semaphore()

    def greet(device):
        pl.semaphore_signal(barrier, inc=1, device_id=device, device_id_type=MESH)

    for step in range(1, n_z):
        greet({"gy": my, "gz": lax.rem(mz + step, n_z)})

    @pl.when(has_low)
    def _():
        for z in (mz, left, right):
            greet({"gy": low, "gz": z})

    @pl.when(has_high)
    def _():
        for z in (mz, left, right):
            greet({"gy": high, "gz": z})

    horizontal(window, False)
    horizontal(window_parted, True)
    for load in loads:
        load.wait()

    heights[...] = jnp.zeros_like(heights)
    heights[0:1, 0:planes] = height[...]
    heights[3:5, 0:planes] = reach[...].astype(jnp.float32)
    lane = lax.broadcasted_iota(jnp.int32, (planes, LANES), 1)
    sub = lax.broadcasted_iota(jnp.int32, (planes, LANES), 0)
    offset = my * planes
    column = offset + jnp.where(
        lane < planes, lane, jnp.where(lane < planes + HMAX, lane - planes - HMAX, lane - HMAX)
    )
    eye = lane == sub

    def upright(k):
        spread = jnp.where(eye, jnp.broadcast_to(heights[k : k + 1, :], (planes, LANES)), 0.0)
        return jnp.sum(spread, axis=1, keepdims=True).astype(jnp.int32)

    plane = offset + lax.broadcasted_iota(jnp.int32, (planes, 1), 0)
    lowest = jnp.maximum(plane - upright(3), 0)
    highest = jnp.minimum(plane + upright(4), n_y * planes - 1)
    allowed = (column >= lowest) & (column <= highest) & (lane < all_planes)
    inside[...] = jnp.where(allowed, 1.0, 0.0)

    for c in range(6):
        send_s[0, c] = strain[c, 0:ROWS, :].astype(jnp.float32)[0:HMAX]
        send_s[1, c] = strain[c, planes - ROWS : planes, :].astype(jnp.float32)[HMAX:ROWS]

    partners = (
        (n_z - 1)
        + 3 * has_low.astype(jnp.int32)
        + 3 * has_high.astype(jnp.int32)
    )
    pl.semaphore_wait(barrier, partners)

    def remote(src, dst, index, device):
        return pltpu.make_async_remote_copy(
            src_ref=src,
            dst_ref=dst,
            send_sem=send_sem.at[index],
            recv_sem=recv_sem.at[index],
            device_id=device,
            device_id_type=MESH,
        )

    top = slice(planes - HMAX, planes)
    under = slice(planes, planes + HMAX)
    over = slice(planes + HMAX, planes + 2 * HMAX)

    def to_high():
        here = {"gy": high, "gz": mz}
        return [
            remote(vel_hbm.at[:, top, :], halo_u.at[:, 0:HMAX, :], 0, here),
            remote(send_s.at[1], halo_s.at[:, 0:HMAX, :], 1, here),
            remote(height_hbm, halo_heights.at[0], 2, here),
            remote(strips.at[0, top, :], halo_strips.at[1, under, :], 3, {"gy": high, "gz": left}),
            remote(strips.at[1, top, :], halo_strips.at[0, under, :], 4, {"gy": high, "gz": right}),
        ]

    def to_low():
        here = {"gy": low, "gz": mz}
        return [
            remote(vel_hbm.at[:, 0:HMAX, :], halo_u.at[:, HMAX : 2 * HMAX, :], 5, here),
            remote(send_s.at[0], halo_s.at[:, HMAX : 2 * HMAX, :], 6, here),
            remote(height_hbm, halo_heights.at[1], 7, here),
            remote(strips.at[0, 0:HMAX, :], halo_strips.at[1, over, :], 8, {"gy": low, "gz": left}),
            remote(strips.at[1, 0:HMAX, :], halo_strips.at[0, over, :], 9, {"gy": low, "gz": right}),
        ]

    def to_sides():
        return [
            remote(strips.at[0], halo_strips.at[1, 0:planes, :], 10, {"gy": my, "gz": left}),
            remote(strips.at[1], halo_strips.at[0, 0:planes, :], 11, {"gy": my, "gz": right}),
        ]

    @pl.when(has_high)
    def _():
        for copy in to_high()[:3]:
            copy.start()

    @pl.when(has_low)
    def _():
        for copy in to_low()[:3]:
            copy.start()

    def pack(i, carry):
        rows = pl.ds(pl.multiple_of(i * ROWS, ROWS), ROWS)
        lane = lane_index(ROWS)
        first = jnp.zeros((ROWS, LANES), jnp.float32)
        last = first
        for g in range(9):
            def tile(start):
                if g < 3:
                    return vel[g, rows, start : start + LANES]
                return strain[g - 3, rows, start : start + LANES].astype(jnp.float32)

            here = (lane >= g * NX) & (lane < (g + 1) * NX)
            a = tile(0)
            b = tile(cells - LANES)
            first = jnp.where(here, pltpu.roll(a, g * NX, 1) if g else a, first)
            last = jnp.where(here, pltpu.roll(b, (g + 1) * NX, 1), last)
        strips[0, rows, :] = first
        strips[1, rows, :] = last
        return carry

    lax.fori_loop(0, planes // ROWS, pack, 0)

    def clear(side):
        span = slice(side * HMAX, (side + 1) * HMAX)
        halo_u[:, span, :] = jnp.zeros((3, HMAX, cells), jnp.float32)
        halo_s[:, span, :] = jnp.zeros((6, HMAX, cells), jnp.float32)
        halo_heights[side] = jnp.zeros(halo_heights.shape[1:], jnp.float32)
        start = planes + side * HMAX
        halo_strips[:, start : start + HMAX, :] = jnp.zeros((2, HMAX, LANES), jnp.float32)

    pl.when(jnp.logical_not(has_low))(lambda: clear(0))
    pl.when(jnp.logical_not(has_high))(lambda: clear(1))

    def form_block(load_u, load_s, start):
        rows = pl.ds(start, ROWS)
        low_rows = pl.ds(start + all_planes, ROWS)
        for t in range(tiles):
            lanes = slice(t * LANES, (t + 1) * LANES)

            def emit(f, x):
                hi, lo = halves(x)
                pieces[f, rows, lanes] = hi
                pieces[f, low_rows, lanes] = lo

            s = [load_s(c, lanes) for c in range(6)]
            rate = strain_rate(s)
            for c in range(6):
                emit(9 + c, rate * s[c])
            u = [load_u(c, lanes) for c in range(3)]
            for c in range(3):
                emit(c, u[c])
            for k in range(6):
                emit(3 + k, u[LEAD_INDEX[k]] * u[TAIL_INDEX[k]])

    def own_block(i, carry):
        start = pl.multiple_of(i * ROWS, ROWS)
        rows = pl.ds(start, ROWS)
        form_block(
            lambda c, lanes: vel[c, rows, lanes],
            lambda c, lanes: strain[c, rows, lanes].astype(jnp.float32),
            start,
        )
        return carry

    @pl.when(has_high)
    def _():
        for copy in to_high()[3:]:
            copy.start()

    @pl.when(has_low)
    def _():
        for copy in to_low()[3:]:
            copy.start()

    for copy in to_sides():
        copy.start()

    lax.fori_loop(0, planes // ROWS, own_block, 0)

    @pl.when(has_low)
    def _():
        for copy in to_high()[:3]:
            copy.wait_recv()

    @pl.when(has_high)
    def _():
        for copy in to_low()[:3]:
            copy.wait_recv()

    form_block(
        lambda c, lanes: halo_u[c, :, lanes],
        lambda c, lanes: halo_s[c, :, lanes],
        planes,
    )
    for c in range(6):
        strain[c, planes:all_planes, :] = halo_s[c].astype(jnp.bfloat16)

    heights[1:2, 0:planes] = halo_heights[0]
    heights[2:3, 0:planes] = halo_heights[1]
    own_row = heights[0:1, :]
    below_row = pltpu.roll(heights[1:2, :], LANES + planes - (planes - HMAX) - LANES, 1)
    above_row = pltpu.roll(heights[2:3, :], planes + HMAX, 1)
    lane_row = lax.broadcasted_iota(jnp.int32, (1, LANES), 1)
    row = jnp.where(
        lane_row < planes,
        own_row,
        jnp.where(lane_row < planes + HMAX, below_row, above_row),
    )
    weights = jnp.broadcast_to(row, (planes, LANES)) * inside[...]
    weights = weights / jnp.sum(weights, axis=1, keepdims=True) * (1.0 / 16.0)
    weights = weights[:, :all_planes]
    w_hi, w_lo = halves(weights)
    exact = jnp.concatenate([w_hi, w_lo], axis=0)
    matrix = jnp.concatenate(
        [
            jnp.concatenate([w_hi, w_hi], axis=1),
            jnp.concatenate([w_lo, jnp.zeros_like(w_lo)], axis=1),
        ],
        axis=0,
    )

    def band(weights, x):
        both = jnp.dot(weights, x, preferred_element_type=jnp.float32)
        return both[:planes] + both[planes:]


    def packed_edges():
        @pl.when(has_low)
        def _():
            for copy in to_high()[3:]:
                copy.wait_recv()

        @pl.when(has_high)
        def _():
            for copy in to_low()[3:]:
                copy.wait_recv()

        for copy in to_sides():
            copy.wait_recv()

        group = lane_index(all_planes) // NX
        scale = jnp.where(group < 3, 0.0, jnp.where(group < 6, 2.0, 4.0))
        for side in range(2):
            x = halo_strips[side]
            squares = x * x
            total = scale * squares
            for shift in (8, 16, 32, 64):
                total = total + pltpu.roll(total, shift, 1)
            rate = jnp.sqrt(total)
            one = pltpu.roll(x * pltpu.roll(x, NX, 1), 64, 1)
            two = pltpu.roll(x * pltpu.roll(x, 2 * NX, 1), 72, 1)
            second = jnp.where(
                group < 3,
                squares,
                jnp.where(group < 9, rate * x, jnp.where(group < 11, one, two)),
            )
            second = jnp.where(group < 12, second, 0.0)
            for k, y in enumerate((x, second)):
                hi, lo = halves(streamwise4(y))
                at = (2 * side + k) * LANES
                packed_pieces[0:all_planes, at : at + LANES] = hi
                packed_pieces[all_planes : 2 * all_planes, at : at + LANES] = lo
        packed_out[...] = band(matrix, packed_pieces[...])


    acc[...] = jnp.zeros_like(acc)
    width = 2 * LANES
    for f in range(FIELDS):
        rows = slice(f * planes, (f + 1) * planes)
        for start in range(0, cells, width):
            lanes = slice(start, start + width)
            if 9 <= f < 15:
                x = band(exact, strain[f - 9, :, lanes])
            else:
                x = band(matrix, pieces[f if f < 9 else f - 6, :, lanes])
            hi, lo = halves(x)
            wall[rows, lanes] = hi
            wall[rows, cells + start : cells + start + width] = lo

    for chunk in range(cells // width):
        last = chunk == cells // width - 1
        along = window_parted if last else window
        for f in range(0, FIELDS, 7):
            rows = slice(f * planes, (f + 7) * planes)
            columns = []
            for base in (0, cells):
                first = base + chunk * width
                if last:
                    columns.append(wall[rows, first : first + width])
                    columns.append(wall[rows, base : base + LANES])
                else:
                    columns.append(wall[rows, first : first + 3 * LANES])
            x = jnp.dot(
                jnp.concatenate(columns, axis=1),
                along[...],
                preferred_element_type=jnp.float32,
            )
            filt[chunk, f : f + 7] = x.reshape(7, planes, width)
        if last:
            packed_edges()
            half = LANES // 2
            for f in range(FIELDS):
                t, g = PACKED_AT[f]
                x = packed_out[:, t * LANES : (t + 1) * LANES]
                y = packed_out[:, (2 + t) * LANES : (3 + t) * LANES]
                x = pltpu.roll(x, (half - NX * g) % LANES, 1) if half != NX * g else x
                shift = (half - NX - NX * g) % LANES
                y = pltpu.roll(y, shift, 1) if shift else y
                x = jnp.where(
                    (lane >= half) & (lane < half + NX),
                    x,
                    jnp.where((lane >= half - NX) & (lane < half), y, 0.0),
                )
                filt[chunk, f, :, LANES:width] = filt[chunk, f, :, LANES:width] + x

        def contract(start):
            rows = slice(start, start + ROWS)
            numerator = jnp.zeros((ROWS, width), jnp.float32)
            denominator = jnp.zeros((ROWS, width), jnp.float32)
            tensor = [filt[chunk, 9 + c, rows, :] for c in range(6)]
            rate = 4.0 * strain_rate(tensor)
            for k in range(6):
                leonard = filt[chunk, 3 + k, rows, :] - filt[chunk, LEAD_INDEX[k], rows, :] * filt[chunk, TAIL_INDEX[k], rows, :]
                model = filt[chunk, 15 + k, rows, :] - rate * tensor[k]
                weighted = model if TENSOR_WEIGHTS[k] == 1.0 else TENSOR_WEIGHTS[k] * model
                numerator = numerator + leonard * weighted
                denominator = denominator + model * weighted
            for t in range(width // LANES):
                at = slice(t * LANES, (t + 1) * LANES)
                acc[rows, 0:LANES] = acc[rows, 0:LANES] + numerator[:, at]
                acc[rows, LANES : 2 * LANES] = acc[rows, LANES : 2 * LANES] + denominator[:, at]

        for start in range(0, planes, ROWS):
            contract(start)

    pick_row = lax.broadcasted_iota(jnp.int32, (8, 2 * LANES), 0)
    pick_lane = lax.broadcasted_iota(jnp.int32, (8, 2 * LANES), 1)
    pick = jnp.where(pick_row == pick_lane // LANES, 1.0, 0.0)
    part[...] = lax.dot_general(
        pick,
        acc[...],
        (((1,), (1,)), ((), ())),
        precision=lax.Precision.HIGHEST,
        preferred_element_type=jnp.float32,
    )
    slots[pl.ds(mz, 1)] = part[...][None]

    def share(step, peer, slot, sem):
        return pltpu.make_async_remote_copy(
            src_ref=part,
            dst_ref=slots.at[slot],
            send_sem=part_send.at[step],
            recv_sem=part_recv.at[sem],
            device_id={"gy": my, "gz": peer},
            device_id_type=MESH,
        )

    for step in range(1, n_z):
        peer = lax.rem(mz + step, n_z)
        share(step, peer, mz, step).start()
    for step in range(1, n_z):
        source = lax.rem(mz + n_z - step, n_z)
        share(step, source, source, step).wait_recv()
    total = jnp.zeros((8, LANES), jnp.float32)
    for k in range(n_z):
        total = total + slots[k]
    count = 1.0 * n_z * cells
    result = total[0:1] / count / (total[1:2] / count + 1e-6)
    out[...] = result[:, :planes]

    for step in range(1, n_z):
        peer = lax.rem(mz + step, n_z)
        share(step, peer, mz, step).wait_send()

    @pl.when(has_high)
    def _():
        for copy in to_high():
            copy.wait_send()

    @pl.when(has_low)
    def _():
        for copy in to_low():
            copy.wait_send()

    for copy in to_sides():
        copy.wait_send()


def local(velocity, strain, cell_height, stencil_reach):
    planes, cells = velocity.shape[1], velocity.shape[2]
    n_y = lax.axis_size("gy")
    n_z = lax.axis_size("gz")
    all_planes = planes + 2 * HMAX
    f32, bf16 = jnp.float32, jnp.bfloat16
    vmem = pl.BlockSpec(memory_space=pltpu.VMEM)
    result = pl.pallas_call(
        functools.partial(kernel, n_y, n_z),
        out_shape=jax.ShapeDtypeStruct((1, planes), f32),
        in_specs=[pl.BlockSpec(memory_space=pltpu.HBM)] * 4,
        out_specs=vmem,
        scratch_shapes=[
            pltpu.VMEM((3, planes, cells), f32),
            pltpu.VMEM((6, all_planes, cells), bf16),
            pltpu.VMEM((1, planes), f32),
            pltpu.VMEM((2, planes), jnp.int32),
            pltpu.VMEM((FIELDS - 6, 2 * all_planes, cells), bf16),
            pltpu.VMEM((FIELDS * planes, 2 * cells), bf16),
            pltpu.VMEM((6 * LANES, 2 * LANES), bf16),
            pltpu.VMEM((6 * LANES, 2 * LANES), bf16),
            pltpu.VMEM((2 * all_planes, 4 * LANES), bf16),
            pltpu.VMEM((planes, 4 * LANES), f32),
            pltpu.VMEM((cells // (2 * LANES), FIELDS, planes, 2 * LANES), f32),
            pltpu.VMEM((3, 2 * HMAX, cells), f32),
            pltpu.VMEM((6, 2 * HMAX, cells), f32),
            pltpu.VMEM((2, 6, HMAX, cells), f32),
            pltpu.VMEM((2, planes, LANES), f32),
            pltpu.VMEM((2, all_planes, LANES), f32),
            pltpu.VMEM((8, LANES), f32),
            pltpu.VMEM((2, 1, planes), f32),
            pltpu.VMEM((LANES, 2 * LANES), f32),
            pltpu.VMEM((8, LANES), f32),
            pltpu.VMEM((n_z, 8, LANES), f32),
            pltpu.SemaphoreType.DMA((12,)),
            pltpu.SemaphoreType.DMA((12,)),
            pltpu.SemaphoreType.DMA((n_z,)),
            pltpu.SemaphoreType.DMA((n_z,)),
            pltpu.SemaphoreType.DMA((4,)),
            pltpu.VMEM((planes, LANES), f32),
        ],
        compiler_params=pltpu.CompilerParams(
            collective_id=0, has_side_effects=True, vmem_limit_bytes=48 * 1024 * 1024
        ),
    )(velocity, strain, cell_height.reshape(1, planes), stencil_reach)
    return result.reshape(planes)


def solution(mesh):
    in_specs = (P(None, "gy", "gz"), P(None, "gy", "gz"), P("gy"), P(None, "gy"))
    return jax.shard_map(local, mesh=mesh, in_specs=in_specs, out_specs=P("gy"), check_vma=False)
```

profile of v0, /device:TPU:1, one launch (start us, length us, event | category | flops | bytes accessed | tf_op | source)
XLA Modules:
  0.0 23.0 jit_solution(15268890691553848245)
XLA Ops:
  0.0 0.0 copy-start.2
  0.0 0.0 copy-start.3
  0.0 0.7 %copy-done.2 = s32[2,96]{1,0:T(2,128)S(1)} copy-done((s32[2,96]{1,0:T(2,128)S(1)}, s32[2,96]{1,0:T(2,128)}, u32[]{:S(2)}) %copy-start.2) | copy-done | bytes 792
  0.7 0.0 copy-done.3
  0.7 0.0 copy-start
  0.7 1.2 %copy-done = f32[3,96,768]{2,1,0:T(8,128)S(1)} copy-done((f32[3,96,768]{2,1,0:T(8,128)S(1)}, f32[3,96,768]{2,1,0:T(8,128)}, u32[]{:S(2)}) %copy-start) | copy-done | bytes 884760
  1.9 0.0 copy-start.1
  1.9 1.2 %copy-done.1 = bf16[6,96,768]{2,1,0:T(8,128)(2,1)S(1)} copy-done((bf16[6,96,768]{2,1,0:T(8,128)(2,1)S(1)}, bf16[6,96,768]{2,1,0:T(8,128)(2,1)}, u32[]{:S(2)}) %copy-start.1) | copy-done | bytes 884760
  3.0 19.4 %shard_map.46 = f32[1,96]{1,0:T(1,128)S(1)} custom-call(f32[3,96,768]{2,1,0:T(8,128)S(1)} %copy-done, bf16[6,96,768]{2,1,0:T(8,128)(2,1)S(1)} %copy-done.1, f32[1,96]{1,0:T(1,128)S(1)} %bitcast.2, s32[2,96]{1,0:T(2,128)S(1)} %copy-done.2), custom_call_target="tpu_custom_call" | custom-call | tf_op jit(solution)/shard_map/pallas_call | solution.py:525
  22.5 0.5 %copy.6 = f32[96]{0:T(128)} copy(f32[96]{0:T(128)S(1)} %bitcast.3) | data formatting | bytes 768
Async XLA Ops:
  0.0 0.7 %copy-start.2 = (s32[2,96]{1,0:T(2,128)S(1)}, s32[2,96]{1,0:T(2,128)}, u32[]{:S(2)}) copy-start(s32[2,96]{1,0:T(2,128)} %reach_hbm.1) | copy-start | bytes 2308
  0.0 0.7 %copy-start.3 = (f32[96]{0:T(128)S(1)}, f32[96]{0:T(128)}, u32[]{:S(2)}) copy-start(f32[96]{0:T(128)} %param.6) | copy-start | bytes 1156
  0.7 1.2 %copy-start = (f32[3,96,768]{2,1,0:T(8,128)S(1)}, f32[3,96,768]{2,1,0:T(8,128)}, u32[]{:S(2)}) copy-start(f32[3,96,768]{2,1,0:T(8,128)} %vel_hbm.1) | copy-start | bytes 2654212
  1.9 1.2 %copy-start.1 = (bf16[6,96,768]{2,1,0:T(8,128)(2,1)S(1)}, bf16[6,96,768]{2,1,0:T(8,128)(2,1)}, u32[]{:S(2)}) copy-start(bf16[6,96,768]{2,1,0:T(8,128)(2,1)} %strain_hbm.1) | copy-start | bytes 2654212
where the time goes:
time: 23.2 us; the launch traced here: 23 us
  Pallas kernels  19.4 us (84%)
  local copies, waits for them, and re-layouts  3.53 us (15%)
    pallas_call x1, Pallas kernels, local(): pl.pallas_call(functools.partial(kernel, n_y, n_z), out_shape=jax.ShapeDt...  19.4 us
    unnamed x9, local copies, waits for them, and re-layouts  3.53 us

commit v1 on v0

--- a/solution.py
+++ b/solution.py
@@ -557,7 +557,7 @@
             pltpu.VMEM((planes, LANES), f32),
         ],
         compiler_params=pltpu.CompilerParams(
-            collective_id=0, has_side_effects=True, vmem_limit_bytes=48 * 1024 * 1024
+            collective_id=0, has_side_effects=True, vmem_limit_bytes=67043328
         ),
     )(velocity, strain, cell_height.reshape(1, planes), stencil_reach)
     return result.reshape(planes)

time: 23.2 us -> 22.2 us (0.957)
  local copies, waits for them, and re-layouts: 3.53 us -> 1.1 us
  Pallas kernels: 19.4 us -> 21 us
    unnamed x9 -> x3, local copies, waits for them, and re-layouts: 3.53 us -> 1.1 us
    pallas_call x1, Pallas kernels: 19.4 us -> 21 us  [local(): pl.pallas_call(functools.partial(kernel, n_y, n_z), out_shape=jax.ShapeDt...]
where the time goes in v1:
time: 22.2 us; the launch traced here: 22.1 us
  Pallas kernels  21 us (95%)
  local copies, waits for them, and re-layouts  1.1 us (5%)
    pallas_call x1, Pallas kernels, local(): pl.pallas_call(functools.partial(kernel, n_y, n_z), out_shape=jax.ShapeDt...  21 us
    unnamed x3, local copies, waits for them, and re-layouts  1.1 us

profile of v1, /device:TPU:1, one launch (start us, length us, event | category | flops | bytes accessed | tf_op | source)
XLA Modules:
  0.0 22.1 jit_solution(14537925214464366049)
XLA Ops:
  0.0 21.0 %shard_map.46 = f32[1,96]{1,0:T(1,128)} custom-call(f32[3,96,768]{2,1,0:T(8,128)} %vel_hbm.1, bf16[6,96,768]{2,1,0:T(8,128)(2,1)} %strain_hbm.1, f32[1,96]{1,0:T(1,128)} %bitcast.2, s32[2,96]{1,0:T(2,128)} %reach_hbm.1), custom_call_target="tpu_custom_call" | custom-call | tf_op jit(solution)/shard_map/pallas_call | solution.py:525
  21.0 0.0 copy-start
  21.0 0.6 %copy-done = f32[1,96]{1,0:T(1,128)S(1)} copy-done((f32[1,96]{1,0:T(1,128)S(1)}, f32[1,96]{1,0:T(1,128)}, u32[]{:S(2)}) %copy-start) | copy-done | bytes 408
  21.6 0.5 %copy.6 = f32[96]{0:T(128)} copy(f32[96]{0:T(128)S(1)} %bitcast.3) | data formatting | bytes 768
Async XLA Ops:
  21.0 0.6 %copy-start = (f32[1,96]{1,0:T(1,128)S(1)}, f32[1,96]{1,0:T(1,128)}, u32[]{:S(2)}) copy-start(f32[1,96]{1,0:T(1,128)} %shard_map.46) | copy-start | bytes 1156

commit v2 on v1

v2 whole, which is shorter than its diff:
```python
import functools

import jax
import jax.numpy as jnp
from jax import lax
from jax.experimental import pallas as pl
from jax.experimental.pallas import tpu as pltpu
from jax.sharding import PartitionSpec as P

NX = 8
HMAX = 8
LANES = 128
ROWS = 16

LEAD_INDEX = (0, 1, 2, 0, 0, 1)
TAIL_INDEX = (0, 1, 2, 1, 2, 2)
TENSOR_WEIGHTS = (1.0, 1.0, 1.0, 2.0, 2.0, 2.0)
FIELDS = 21
PACKED_AT = (
    [(0, 6), (0, 7), (2, 0)]
    + [(1, 6), (1, 7), (2, 1), (2, 5), (2, 6), (2, 7)]
    + [(0, c) for c in range(6)]
    + [(1, c) for c in range(6)]
)
MESH = pl.DeviceIdType.MESH


def strain_rate(t):
    squares = 2.0 * (t[0] * t[0] + t[1] * t[1] + t[2] * t[2])
    return jnp.sqrt(squares + 4.0 * (t[3] * t[3] + t[4] * t[4] + t[5] * t[5]))


def lane_index(rows):
    return lax.broadcasted_iota(jnp.int32, (rows, LANES), 1)


def streamwise4(x):
    position = lane_index(x.shape[0]) % NX
    behind = jnp.where(
        position == 0, pltpu.roll(x, LANES + 1 - NX, 1), pltpu.roll(x, 1, 1)
    )
    ahead = jnp.where(
        position == NX - 1, pltpu.roll(x, NX - 1, 1), pltpu.roll(x, LANES - 1, 1)
    )
    return behind + ahead + (x + x)


def horizontal(window, parted):
    shape = (3 * LANES, 2 * LANES)
    source = lax.broadcasted_iota(jnp.int32, shape, 0)
    target = lax.broadcasted_iota(jnp.int32, shape, 1) + LANES // 2
    cells_apart = jnp.abs(source // NX - target // NX)
    along = (source - target) & (NX - 1)
    span = jnp.where(cells_apart == 0, 2.0, jnp.where(cells_apart == 1, 1.0, 0.0))
    stream = jnp.where(along == 0, 2.0, jnp.where((along == 1) | (along == NX - 1), 1.0, 0.0))
    both = span * stream
    if parted:
        both = jnp.where((source < 2 * LANES) == (target < 2 * LANES), both, 0.0)
    both = both.astype(jnp.bfloat16)
    window[0 : 3 * LANES, :] = both
    window[3 * LANES : 6 * LANES, :] = both


def halves(x):
    high = x.astype(jnp.bfloat16)
    return high, (x - high.astype(jnp.float32)).astype(jnp.bfloat16)


def kernel(
    n_y,
    n_z,
    vel_hbm,
    strain_hbm,
    height_hbm,
    reach_hbm,
    out,
    vel,
    strain,
    height,
    reach,
    pieces,
    halo_pieces,
    wall,
    wall_rim,
    rim,
    window,
    window_parted,
    packed_pieces,
    packed_out,
    filt,
    halo_u,
    halo_s,
    halo_strain,
    send_s,
    strips,
    halo_strips,
    heights,
    halo_heights,
    upright_height,
    norm,
    acc,
    part,
    slots,
    send_sem,
    recv_sem,
    part_send,
    part_recv,
    load_sem,
    inside,
):
    planes, cells = vel.shape[1], vel.shape[2]
    all_planes = planes + 2 * HMAX
    inner = planes - 2 * HMAX
    bottom = slice(0, ROWS)
    middle = slice(ROWS, planes - ROWS)
    summit = slice(planes - ROWS, planes)
    loads = [
        pltpu.make_async_copy(height_hbm, height, load_sem.at[0]),
        pltpu.make_async_copy(reach_hbm, reach, load_sem.at[1]),
        pltpu.make_async_copy(strain_hbm.at[:, bottom, :], strain.at[:, bottom, :], load_sem.at[2]),
        pltpu.make_async_copy(strain_hbm.at[:, summit, :], strain.at[:, summit, :], load_sem.at[3]),
        pltpu.make_async_copy(vel_hbm, vel, load_sem.at[4]),
        pltpu.make_async_copy(strain_hbm.at[:, middle, :], strain.at[:, middle, :], load_sem.at[5]),
    ]
    for load in loads:
        load.start()
    tiles = cells // LANES
    my = lax.axis_index("gy")
    mz = lax.axis_index("gz")
    right = lax.rem(mz + 1, n_z)
    left = lax.rem(mz + n_z - 1, n_z)
    has_low = my > 0
    has_high = my < n_y - 1
    low = my - 1
    high = my + 1

    barrier = pltpu.get_barrier_semaphore()

    def greet(device):
        pl.semaphore_signal(barrier, inc=1, device_id=device, device_id_type=MESH)

    for step in range(1, n_z):
        greet({"gy": my, "gz": lax.rem(mz + step, n_z)})

    @pl.when(has_low)
    def _():
        for z in (mz, left, right):
            greet({"gy": low, "gz": z})

    @pl.when(has_high)
    def _():
        for z in (mz, left, right):
            greet({"gy": high, "gz": z})

    horizontal(window, False)
    horizontal(window_parted, True)

    for load in loads[:4]:
        load.wait()
    for c in range(6):
        send_s[0, c] = strain[c, 0:ROWS, :].astype(jnp.float32)[0:HMAX]
        send_s[1, c] = strain[c, planes - ROWS : planes, :].astype(jnp.float32)[HMAX:ROWS]

    heights[...] = jnp.zeros_like(heights)
    heights[0:1, 0:planes] = height[...]
    heights[3:5, 0:planes] = reach[...].astype(jnp.float32)
    lane = lax.broadcasted_iota(jnp.int32, (planes, LANES), 1)
    sub = lax.broadcasted_iota(jnp.int32, (planes, LANES), 0)
    own = jnp.where(sub < inner, sub + HMAX, jnp.where(sub < inner + HMAX, sub - inner, sub))
    offset = my * planes
    column = offset + jnp.where(
        lane < planes, lane, jnp.where(lane < planes + HMAX, lane - planes - HMAX, lane - HMAX)
    )

    def upright(k, at):
        rows = at.shape[0]
        spread = jnp.where(at, jnp.broadcast_to(heights[k : k + 1, :], (rows, LANES)), 0.0)
        return jnp.sum(spread, axis=1, keepdims=True)

    picked = lane == own
    plane = offset + own
    lowest = jnp.maximum(plane - upright(3, picked).astype(jnp.int32), 0)
    highest = jnp.minimum(plane + upright(4, picked).astype(jnp.int32), n_y * planes - 1)
    allowed = (column >= lowest) & (column <= highest) & (lane < all_planes)
    within = jnp.where(allowed, 1.0, 0.0)
    inside[...] = within
    own_row = heights[0:1, :]
    upright_height[0:planes, :] = jnp.broadcast_to(upright(0, lane == sub), (planes, LANES))
    weights = within * own_row
    total = jnp.sum(weights[0:inner], axis=1, keepdims=True)
    norm[0:inner, :] = jnp.broadcast_to((1.0 / 16.0) / total, (inner, LANES))
    mask = within.astype(jnp.bfloat16)
    mask_own = jnp.concatenate([mask[:, :planes]] * 2, axis=1)
    weights_own = jnp.concatenate(halves(weights[:, :planes]), axis=1)

    for load in loads[4:]:
        load.wait()

    def pack(i, carry):
        rows = pl.ds(pl.multiple_of(i * ROWS, ROWS), ROWS)
        lane = lane_index(ROWS)
        first = jnp.zeros((ROWS, LANES), jnp.float32)
        last = first
        for g in range(9):
            def tile(start):
                if g < 6:
                    return strain[g, rows, start : start + LANES].astype(jnp.float32)
                return vel[g - 6, rows, start : start + LANES]

            a = tile(0)
            b = tile(cells - LANES)
            to_first = 2 * g * NX if g < 8 else NX
            to_last = (2 * g + 1) * NX if g < 8 else 0
            a = pltpu.roll(a, to_first, 1) if to_first else a
            move = (to_last + NX) % LANES
            b = pltpu.roll(b, move, 1) if move else b
            first = jnp.where((lane >= to_first) & (lane < to_first + NX), a, first)
            last = jnp.where((lane >= to_last) & (lane < to_last + NX), b, last)
        strips[0, rows, :] = first
        strips[1, rows, :] = last
        return carry

    lax.fori_loop(0, planes // ROWS, pack, 0)

    def form_block(load_u, load_s, height_rows, into, hi_rows, lo_rows):
        h = upright_height[height_rows, :]
        for t in range(tiles):
            lanes = slice(t * LANES, (t + 1) * LANES)

            def emit(f, x):
                hi, lo = halves(x)
                into[f, hi_rows, lanes] = hi
                into[f, lo_rows, lanes] = lo

            s = [load_s(c, lanes) for c in range(6)]
            rate = h * strain_rate(s)
            for c in range(6):
                emit(9 + c, rate * s[c])
            u = [load_u(c, lanes) for c in range(3)]
            hu = [h * x for x in u]
            for c in range(3):
                emit(c, hu[c])
            for k in range(6):
                emit(3 + k, hu[LEAD_INDEX[k]] * u[TAIL_INDEX[k]])

    def own_block(i, carry):
        start = pl.multiple_of(i * ROWS, ROWS)
        rows = pl.ds(start, ROWS)
        form_block(
            lambda c, lanes: vel[c, rows, lanes],
            lambda c, lanes: strain[c, rows, lanes].astype(jnp.float32),
            rows,
            pieces,
            rows,
            pl.ds(start + planes, ROWS),
        )
        return carry

    partners = (
        (n_z - 1)
        + 3 * has_low.astype(jnp.int32)
        + 3 * has_high.astype(jnp.int32)
    )
    pl.semaphore_wait(barrier, partners)

    def remote(src, dst, index, device):
        return pltpu.make_async_remote_copy(
            src_ref=src,
            dst_ref=dst,
            send_sem=send_sem.at[index],
            recv_sem=recv_sem.at[index],
            device_id=device,
            device_id_type=MESH,
        )

    top = slice(planes - HMAX, planes)
    under = slice(planes, planes + HMAX)
    over = slice(planes + HMAX, planes + 2 * HMAX)

    def to_high():
        here = {"gy": high, "gz": mz}
        return [
            remote(height, halo_heights.at[0], 2, here),
            remote(vel_hbm.at[:, top, :], halo_u.at[:, 0:HMAX, :], 0, here),
            remote(send_s.at[1], halo_s.at[:, 0:HMAX, :], 1, here),
            remote(strips.at[0, top, :], halo_strips.at[1, under, :], 3, {"gy": high, "gz": left}),
            remote(strips.at[1, top, :], halo_strips.at[0, under, :], 4, {"gy": high, "gz": right}),
        ]

    def to_low():
        here = {"gy": low, "gz": mz}
        return [
            remote(height, halo_heights.at[1], 7, here),
            remote(vel_hbm.at[:, 0:HMAX, :], halo_u.at[:, HMAX : 2 * HMAX, :], 5, here),
            remote(send_s.at[0], halo_s.at[:, HMAX : 2 * HMAX, :], 6, here),
            remote(strips.at[0, 0:HMAX, :], halo_strips.at[1, over, :], 8, {"gy": low, "gz": left}),
            remote(strips.at[1, 0:HMAX, :], halo_strips.at[0, over, :], 9, {"gy": low, "gz": right}),
        ]

    def to_sides():
        return [
            remote(strips.at[0], halo_strips.at[1, 0:planes, :], 10, {"gy": my, "gz": left}),
            remote(strips.at[1], halo_strips.at[0, 0:planes, :], 11, {"gy": my, "gz": right}),
        ]

    @pl.when(has_high)
    def _():
        for copy in to_high():
            copy.start()

    @pl.when(has_low)
    def _():
        for copy in to_low():
            copy.start()

    for copy in to_sides():
        copy.start()

    def clear(side):
        span = slice(side * HMAX, (side + 1) * HMAX)
        halo_u[:, span, :] = jnp.zeros((3, HMAX, cells), jnp.float32)
        halo_s[:, span, :] = jnp.zeros((6, HMAX, cells), jnp.float32)
        halo_heights[side] = jnp.zeros(halo_heights.shape[1:], jnp.float32)
        start = planes + side * HMAX
        halo_strips[:, start : start + HMAX, :] = jnp.zeros((2, HMAX, LANES), jnp.float32)

    pl.when(jnp.logical_not(has_low))(lambda: clear(0))
    pl.when(jnp.logical_not(has_high))(lambda: clear(1))

    lax.fori_loop(0, planes // ROWS, own_block, 0)

    acc[...] = jnp.zeros_like(acc)
    width = 2 * LANES
    chunks = cells // width

    def put(ref, rows, start, x):
        hi, lo = halves(x)
        ref[rows, start : start + width] = hi
        ref[rows, cells + start : cells + start + width] = lo

    def band(weights, x):
        return jnp.dot(weights, x, preferred_element_type=jnp.float32)

    for f in range(FIELDS):
        for start in range(0, cells, width):
            lanes = slice(start, start + width)
            if 9 <= f < 15:
                s = strain[f - 9, :, lanes]
                x = band(weights_own, jnp.concatenate([s, s], axis=0))
            else:
                x = band(mask_own, pieces[f if f < 9 else f - 6, :, lanes])
            put(wall, slice(f * inner, (f + 1) * inner), start, x[:inner])
            rim[f, :, lanes] = x[inner:]

    def along(ref, rows, chunk):
        last = chunk == chunks - 1
        columns = []
        for base in (0, cells):
            first = base + chunk * width
            if last:
                columns.append(ref[rows, first : first + width])
                columns.append(ref[rows, base : base + LANES])
            else:
                columns.append(ref[rows, first : first + 3 * LANES])
        return jnp.dot(
            jnp.concatenate(columns, axis=1),
            (window_parted if last else window)[...],
            preferred_element_type=jnp.float32,
        )

    def contract(chunk, start, lanes):
        rows = slice(start, start + ROWS)
        q = norm[rows, :]

        def of(f):
            return filt[chunk, f, rows, lanes]

        tensor = [of(9 + c) for c in range(6)]
        rate = 4.0 * q * strain_rate(tensor)
        u = [of(c) for c in range(3)]
        qu = [q * x for x in u]
        sums = [[None, None], [None, None]]
        for k in range(6):
            leonard = of(3 + k) - qu[LEAD_INDEX[k]] * u[TAIL_INDEX[k]]
            model = of(15 + k) - rate * tensor[k]
            group = sums[0 if TENSOR_WEIGHTS[k] == 1.0 else 1]
            for at, term in enumerate((leonard * model, model * model)):
                group[at] = term if group[at] is None else group[at] + term
        for at in range(2):
            span = slice(at * LANES, (at + 1) * LANES)
            acc[rows, span] = acc[rows, span] + (sums[0][at] + 2.0 * sums[1][at])

    def contract_chunk(chunk, starts):
        for start in starts:
            for t in range(2):
                if chunk == chunks - 1 and t == 1:
                    continue
                contract(chunk, start, slice(t * LANES, (t + 1) * LANES))

    step_fields = 7
    for chunk in range(chunks):
        for f in range(0, FIELDS, step_fields):
            x = along(wall, slice(f * inner, (f + step_fields) * inner), chunk)
            filt[chunk, f : f + step_fields, 0:inner] = x.reshape(step_fields, inner, width)
        contract_chunk(chunk, range(0, inner, ROWS))

    @pl.when(has_low)
    def _():
        for copy in to_high()[:3]:
            copy.wait_recv()

    @pl.when(has_high)
    def _():
        for copy in to_low()[:3]:
            copy.wait_recv()

    heights[1:2, 0:planes] = halo_heights[0]
    heights[2:3, 0:planes] = halo_heights[1]
    below_row = pltpu.roll(heights[1:2, :], HMAX, 1)
    above_row = pltpu.roll(heights[2:3, :], planes + HMAX, 1)
    lane_row = lax.broadcasted_iota(jnp.int32, (1, LANES), 1)
    row = jnp.where(
        lane_row < planes,
        heights[0:1, :],
        jnp.where(lane_row < planes + HMAX, below_row, above_row),
    )
    heights[0:1, :] = row
    rim_lane = lax.broadcasted_iota(jnp.int32, (ROWS, LANES), 1)
    rim_sub = lax.broadcasted_iota(jnp.int32, (ROWS, LANES), 0)
    upright_height[planes:all_planes, :] = jnp.broadcast_to(
        upright(0, rim_lane == rim_sub + planes), (ROWS, LANES)
    )
    rim_inside = inside[inner:planes, :]
    rim_weights = rim_inside * row
    norm[inner:planes, :] = jnp.broadcast_to(
        (1.0 / 16.0) / jnp.sum(rim_weights, axis=1, keepdims=True), (ROWS, LANES)
    )
    rim_mask = jnp.concatenate([rim_inside.astype(jnp.bfloat16)[:, planes:all_planes]] * 2, axis=1)
    rim_weights = jnp.concatenate(halves(rim_weights[:, planes:all_planes]), axis=1)

    form_block(
        lambda c, lanes: halo_u[c, :, lanes],
        lambda c, lanes: halo_s[c, :, lanes],
        slice(planes, all_planes),
        halo_pieces,
        slice(0, ROWS),
        slice(ROWS, 2 * ROWS),
    )
    for c in range(6):
        halo_strain[c] = halo_s[c].astype(jnp.bfloat16)

    for f in range(FIELDS):
        for start in range(0, cells, width):
            lanes = slice(start, start + width)
            if 9 <= f < 15:
                s = halo_strain[f - 9, :, lanes]
                x = band(rim_weights, jnp.concatenate([s, s], axis=0))
            else:
                x = band(rim_mask, halo_pieces[f if f < 9 else f - 6, :, lanes])
            put(wall_rim, slice(f * ROWS, (f + 1) * ROWS), start, rim[f, :, lanes] + x)

    for chunk in range(chunks):
        x = along(wall_rim, slice(0, FIELDS * ROWS), chunk)
        filt[chunk, :, inner:planes] = x.reshape(FIELDS, ROWS, width)
        contract_chunk(chunk, [inner])

    @pl.when(has_low)
    def _():
        for copy in to_high()[3:]:
            copy.wait_recv()

    @pl.when(has_high)
    def _():
        for copy in to_low()[3:]:
            copy.wait_recv()

    for copy in to_sides():
        copy.wait_recv()

    strip_lane = lane_index(ROWS)
    group = strip_lane // (2 * NX)
    is_right = strip_lane % (2 * NX) < NX
    scale = jnp.where(group < 3, 2.0, jnp.where(group < 6, 4.0, 0.0))
    for start in range(0, all_planes, ROWS):
        rows = slice(start, start + ROWS)
        low_rows = slice(all_planes + start, all_planes + start + ROWS)
        h = upright_height[rows, :]
        from_left = halo_strips[0, rows, :]
        from_right = halo_strips[1, rows, :]
        a = jnp.where(is_right, from_right, from_left)
        b = jnp.where(is_right, pltpu.roll(from_right, LANES - NX, 1), pltpu.roll(from_left, NX, 1))
        b = jnp.where(group == 0, b, 0.0)
        ha = h * a
        hb = h * b
        total = scale * a * a
        for shift in (16, 32, 64):
            total = total + pltpu.roll(total, shift, 1)
        rate = jnp.sqrt(total)
        u2 = pltpu.roll(b, 6 * 16, 1) + pltpu.roll(b, 7 * 16, 1)
        mixed = pltpu.roll(ha * pltpu.roll(a, LANES - 16, 1), LANES - 16, 1)
        second = jnp.where(group < 6, rate * ha, ha * a)
        third = jnp.where(
            group < 5,
            hb + pltpu.roll(hb * b, 16, 1),
            jnp.where(group == 5, mixed, ha * u2),
        )
        for k, y in enumerate((ha, second, third)):
            hi, lo = halves(y)
            at = slice(k * LANES, (k + 1) * LANES)
            packed_pieces[rows, at] = hi
            packed_pieces[low_rows, at] = lo
    mask_all = inside[...].astype(jnp.bfloat16)[:, :all_planes]
    packed_out[...] = band(jnp.concatenate([mask_all, mask_all], axis=1), packed_pieces[...])

    half = LANES // 2
    joint = (strip_lane >= half - NX) & (strip_lane < half + NX)
    tail = slice(LANES, width)
    for start in range(0, planes, ROWS):
        rows = slice(start, start + ROWS)
        edge = [streamwise4(packed_out[rows, k * LANES : (k + 1) * LANES]) for k in range(3)]
        for f in range(FIELDS):
            t, g = PACKED_AT[f]
            shift = (half - NX - 2 * NX * g) % LANES
            x = pltpu.roll(edge[t], shift, 1) if shift else edge[t]
            filt[chunks - 1, f, rows, tail] = filt[chunks - 1, f, rows, tail] + jnp.where(joint, x, 0.0)
        contract(chunks - 1, start, tail)

    q = norm[...]
    scaled = jnp.concatenate([acc[:, 0:LANES] * (q * q), acc[:, LANES:width] * (q * q)], axis=1)
    pick_row = lax.broadcasted_iota(jnp.int32, (8, 2 * LANES), 0)
    pick_lane = lax.broadcasted_iota(jnp.int32, (8, 2 * LANES), 1)
    pick = jnp.where(pick_row == pick_lane // LANES, 1.0, 0.0)
    part[...] = jnp.zeros_like(part)
    part[:, 0:planes] = lax.dot_general(
        pick,
        scaled,
        (((1,), (1,)), ((), ())),
        precision=lax.Precision.HIGHEST,
        preferred_element_type=jnp.float32,
    )
    slots[pl.ds(mz, 1)] = part[...][None]

    def share(step, peer, slot, sem):
        return pltpu.make_async_remote_copy(
            src_ref=part,
            dst_ref=slots.at[slot],
            send_sem=part_send.at[step],
            recv_sem=part_recv.at[sem],
            device_id={"gy": my, "gz": peer},
            device_id_type=MESH,
        )

    for step in range(1, n_z):
        peer = lax.rem(mz + step, n_z)
        share(step, peer, mz, step).start()
    for step in range(1, n_z):
        source = lax.rem(mz + n_z - step, n_z)
        share(step, source, source, step).wait_recv()
    total = jnp.zeros((8, LANES), jnp.float32)
    for k in range(n_z):
        total = total + slots[k]
    count = 1.0 * n_z * cells
    result = total[0:1] / count / (total[1:2] / count + 1e-6)
    inner_row = pltpu.roll(result, HMAX, 1)
    low_row = pltpu.roll(result, LANES - inner, 1)
    result = jnp.where(
        lane_row < HMAX, low_row, jnp.where(lane_row < planes - HMAX, inner_row, result)
    )
    out[...] = result[:, :planes]

    for step in range(1, n_z):
        peer = lax.rem(mz + step, n_z)
        share(step, peer, mz, step).wait_send()

    @pl.when(has_high)
    def _():
        for copy in to_high():
            copy.wait_send()

    @pl.when(has_low)
    def _():
        for copy in to_low():
            copy.wait_send()

    for copy in to_sides():
        copy.wait_send()


def local(velocity, strain, cell_height, stencil_reach):
    planes, cells = velocity.shape[1], velocity.shape[2]
    n_y = lax.axis_size("gy")
    n_z = lax.axis_size("gz")
    all_planes = planes + 2 * HMAX
    inner = planes - 2 * HMAX
    f32, bf16 = jnp.float32, jnp.bfloat16
    vmem = pl.BlockSpec(memory_space=pltpu.VMEM)
    result = pl.pallas_call(
        functools.partial(kernel, n_y, n_z),
        out_shape=jax.ShapeDtypeStruct((1, planes), f32),
        in_specs=[pl.BlockSpec(memory_space=pltpu.HBM)] * 4,
        out_specs=vmem,
        scratch_shapes=[
            pltpu.VMEM((3, planes, cells), f32),
            pltpu.VMEM((6, planes, cells), bf16),
            pltpu.VMEM((1, planes), f32),
            pltpu.VMEM((2, planes), jnp.int32),
            pltpu.VMEM((FIELDS - 6, 2 * planes, cells), bf16),
            pltpu.VMEM((FIELDS - 6, 2 * ROWS, cells), bf16),
            pltpu.VMEM((FIELDS * inner, 2 * cells), bf16),
            pltpu.VMEM((FIELDS * ROWS, 2 * cells), bf16),
            pltpu.VMEM((FIELDS, ROWS, cells), f32),
            pltpu.VMEM((6 * LANES, 2 * LANES), bf16),
            pltpu.VMEM((6 * LANES, 2 * LANES), bf16),
            pltpu.VMEM((2 * all_planes, 3 * LANES), bf16),
            pltpu.VMEM((planes, 3 * LANES), f32),
            pltpu.VMEM((cells // (2 * LANES), FIELDS, planes, 2 * LANES), f32),
            pltpu.VMEM((3, 2 * HMAX, cells), f32),
            pltpu.VMEM((6, 2 * HMAX, cells), f32),
            pltpu.VMEM((6, 2 * HMAX, cells), bf16),
            pltpu.VMEM((2, 6, HMAX, cells), f32),
            pltpu.VMEM((2, planes, LANES), f32),
            pltpu.VMEM((2, all_planes, LANES), f32),
            pltpu.VMEM((8, LANES), f32),
            pltpu.VMEM((2, 1, planes), f32),
            pltpu.VMEM((all_planes, LANES), f32),
            pltpu.VMEM((planes, LANES), f32),
            pltpu.VMEM((planes, 2 * LANES), f32),
            pltpu.VMEM((8, LANES), f32),
            pltpu.VMEM((n_z, 8, LANES), f32),
            pltpu.SemaphoreType.DMA((12,)),
            pltpu.SemaphoreType.DMA((12,)),
            pltpu.SemaphoreType.DMA((n_z,)),
            pltpu.SemaphoreType.DMA((n_z,)),
            pltpu.SemaphoreType.DMA((6,)),
            pltpu.VMEM((planes, LANES), f32),
        ],
        compiler_params=pltpu.CompilerParams(
            collective_id=0, has_side_effects=True, vmem_limit_bytes=67043328
        ),
    )(velocity, strain, cell_height.reshape(1, planes), stencil_reach)
    return result.reshape(planes)


def solution(mesh):
    in_specs = (P(None, "gy", "gz"), P(None, "gy", "gz"), P("gy"), P(None, "gy"))
    return jax.shard_map(local, mesh=mesh, in_specs=in_specs, out_specs=P("gy"), check_vma=False)
```

time: 22.2 us -> 19.2 us (0.86)
  the two profiles are of different devices: /device:TPU:1 before, /device:TPU:0 now
where the time goes in v2:
time: 19.2 us; the launch traced here: 19 us
  Pallas kernels  17.9 us (93%)
  local copies, waits for them, and re-layouts  1.1 us (6%)
    pallas_call x1, Pallas kernels, local(): pl.pallas_call(functools.partial(kernel, n_y, n_z), out_shape=jax.ShapeDt...  17.9 us
    unnamed x3, local copies, waits for them, and re-layouts  1.1 us

profile of v2, /device:TPU:0, one launch (start us, length us, event | category | flops | bytes accessed | tf_op | source)
XLA Modules:
  0.0 19.0 jit_solution(14656116608217445249)
XLA Ops:
  0.0 17.9 %shard_map.46 = f32[1,96]{1,0:T(1,128)} custom-call(f32[3,96,768]{2,1,0:T(8,128)} %vel_hbm.1, bf16[6,96,768]{2,1,0:T(8,128)(2,1)} %strain_hbm.1, f32[1,96]{1,0:T(1,128)} %bitcast.2, s32[2,96]{1,0:T(2,128)} %reach_hbm.1), custom_call_target="tpu_custom_call" | custom-call | tf_op jit(solution)/shard_map/pallas_call | solution.py:597
  17.9 0.0 copy-start
  17.9 0.6 %copy-done = f32[1,96]{1,0:T(1,128)S(1)} copy-done((f32[1,96]{1,0:T(1,128)S(1)}, f32[1,96]{1,0:T(1,128)}, u32[]{:S(2)}) %copy-start) | copy-done | bytes 408
  18.5 0.5 %copy.6 = f32[96]{0:T(128)} copy(f32[96]{0:T(128)S(1)} %bitcast.3) | data formatting | bytes 768
Async XLA Ops:
  17.9 0.6 %copy-start = (f32[1,96]{1,0:T(1,128)S(1)}, f32[1,96]{1,0:T(1,128)}, u32[]{:S(2)}) copy-start(f32[1,96]{1,0:T(1,128)} %shard_map.46) | copy-start | bytes 1156

commit v3 on v2

--- a/solution.py
+++ b/solution.py
@@ -86,11 +86,11 @@
     window,
     window_parted,
     packed_pieces,
+    rim_packed,
     packed_out,
     filt,
     halo_u,
     halo_s,
-    halo_strain,
     send_s,
     strips,
     halo_strips,
@@ -222,20 +222,29 @@
 
     lax.fori_loop(0, planes // ROWS, pack, 0)
 
-    def form_block(load_u, load_s, height_rows, into, hi_rows, lo_rows):
+    def emit_to(into, hi_rows, lo_rows, lanes):
+        def emit(f, x):
+            hi, lo = halves(x)
+            into[f, hi_rows, lanes] = hi
+            into[f, lo_rows, lanes] = lo
+
+        return emit
+
+    def form_rates(load_s, height_rows, into, hi_rows, lo_rows):
         h = upright_height[height_rows, :]
         for t in range(tiles):
             lanes = slice(t * LANES, (t + 1) * LANES)
-
-            def emit(f, x):
-                hi, lo = halves(x)
-                into[f, hi_rows, lanes] = hi
-                into[f, lo_rows, lanes] = lo
-
+            emit = emit_to(into, hi_rows, lo_rows, lanes)
             s = [load_s(c, lanes) for c in range(6)]
             rate = h * strain_rate(s)
             for c in range(6):
                 emit(9 + c, rate * s[c])
+
+    def form_flow(load_u, height_rows, into, hi_rows, lo_rows):
+        h = upright_height[height_rows, :]
+        for t in range(tiles):
+            lanes = slice(t * LANES, (t + 1) * LANES)
+            emit = emit_to(into, hi_rows, lo_rows, lanes)
             u = [load_u(c, lanes) for c in range(3)]
             hu = [h * x for x in u]
             for c in range(3):
@@ -246,15 +255,14 @@
     def own_block(i, carry):
         start = pl.multiple_of(i * ROWS, ROWS)
         rows = pl.ds(start, ROWS)
-        form_block(
-            lambda c, lanes: vel[c, rows, lanes],
-            lambda c, lanes: strain[c, rows, lanes].astype(jnp.float32),
-            rows,
-            pieces,
-            rows,
-            pl.ds(start + planes, ROWS),
-        )
+        places = (rows, pieces, rows, pl.ds(start + planes, ROWS))
+        form_rates(lambda c, lanes: strain[c, rows, lanes].astype(jnp.float32), *places)
+        form_flow(lambda c, lanes: vel[c, rows, lanes], *places)
         return carry
+
+    blocks = planes // ROWS
+    early = blocks - blocks // 3
+    lax.fori_loop(0, early, own_block, 0)
 
     partners = (
         (n_z - 1)
@@ -327,7 +335,7 @@
     pl.when(jnp.logical_not(has_low))(lambda: clear(0))
     pl.when(jnp.logical_not(has_high))(lambda: clear(1))
 
-    lax.fori_loop(0, planes // ROWS, own_block, 0)
+    lax.fori_loop(early, blocks, own_block, 0)
 
     acc[...] = jnp.zeros_like(acc)
     width = 2 * LANES
@@ -368,8 +376,9 @@
             preferred_element_type=jnp.float32,
         )
 
-    def contract(chunk, start, lanes):
-        rows = slice(start, start + ROWS)
+    def contract(chunk, start, t):
+        rows = slice(start, start + 8)
+        lanes = slice(t * LANES, (t + 1) * LANES)
         q = norm[rows, :]
 
         def of(f):
@@ -390,89 +399,21 @@
             span = slice(at * LANES, (at + 1) * LANES)
             acc[rows, span] = acc[rows, span] + (sums[0][at] + 2.0 * sums[1][at])
 
-    def contract_chunk(chunk, starts):
-        for start in starts:
-            for t in range(2):
-                if chunk == chunks - 1 and t == 1:
-                    continue
-                contract(chunk, start, slice(t * LANES, (t + 1) * LANES))
-
-    step_fields = 7
+    def jobs(chunk, first, stop):
+        parts = [0] if chunk == chunks - 1 else [0, 1]
+        return [(chunk, start, t) for start in range(first, stop, 8) for t in parts]
+
+    step_fields = 3
+    pending = []
     for chunk in range(chunks):
+        share_of = -(-len(pending) // (FIELDS // step_fields))
         for f in range(0, FIELDS, step_fields):
             x = along(wall, slice(f * inner, (f + step_fields) * inner), chunk)
             filt[chunk, f : f + step_fields, 0:inner] = x.reshape(step_fields, inner, width)
-        contract_chunk(chunk, range(0, inner, ROWS))
-
-    @pl.when(has_low)
-    def _():
-        for copy in to_high()[:3]:
-            copy.wait_recv()
-
-    @pl.when(has_high)
-    def _():
-        for copy in to_low()[:3]:
-            copy.wait_recv()
-
-    heights[1:2, 0:planes] = halo_heights[0]
-    heights[2:3, 0:planes] = halo_heights[1]
-    below_row = pltpu.roll(heights[1:2, :], HMAX, 1)
-    above_row = pltpu.roll(heights[2:3, :], planes + HMAX, 1)
-    lane_row = lax.broadcasted_iota(jnp.int32, (1, LANES), 1)
-    row = jnp.where(
-        lane_row < planes,
-        heights[0:1, :],
-        jnp.where(lane_row < planes + HMAX, below_row, above_row),
-    )
-    heights[0:1, :] = row
-    rim_lane = lax.broadcasted_iota(jnp.int32, (ROWS, LANES), 1)
-    rim_sub = lax.broadcasted_iota(jnp.int32, (ROWS, LANES), 0)
-    upright_height[planes:all_planes, :] = jnp.broadcast_to(
-        upright(0, rim_lane == rim_sub + planes), (ROWS, LANES)
-    )
-    rim_inside = inside[inner:planes, :]
-    rim_weights = rim_inside * row
-    norm[inner:planes, :] = jnp.broadcast_to(
-        (1.0 / 16.0) / jnp.sum(rim_weights, axis=1, keepdims=True), (ROWS, LANES)
-    )
-    rim_mask = jnp.concatenate([rim_inside.astype(jnp.bfloat16)[:, planes:all_planes]] * 2, axis=1)
-    rim_weights = jnp.concatenate(halves(rim_weights[:, planes:all_planes]), axis=1)
-
-    form_block(
-        lambda c, lanes: halo_u[c, :, lanes],
-        lambda c, lanes: halo_s[c, :, lanes],
-        slice(planes, all_planes),
-        halo_pieces,
-        slice(0, ROWS),
-        slice(ROWS, 2 * ROWS),
-    )
-    for c in range(6):
-        halo_strain[c] = halo_s[c].astype(jnp.bfloat16)
-
-    for f in range(FIELDS):
-        for start in range(0, cells, width):
-            lanes = slice(start, start + width)
-            if 9 <= f < 15:
-                s = halo_strain[f - 9, :, lanes]
-                x = band(rim_weights, jnp.concatenate([s, s], axis=0))
-            else:
-                x = band(rim_mask, halo_pieces[f if f < 9 else f - 6, :, lanes])
-            put(wall_rim, slice(f * ROWS, (f + 1) * ROWS), start, rim[f, :, lanes] + x)
-
-    for chunk in range(chunks):
-        x = along(wall_rim, slice(0, FIELDS * ROWS), chunk)
-        filt[chunk, :, inner:planes] = x.reshape(FIELDS, ROWS, width)
-        contract_chunk(chunk, [inner])
-
-    @pl.when(has_low)
-    def _():
-        for copy in to_high()[3:]:
-            copy.wait_recv()
-
-    @pl.when(has_high)
-    def _():
-        for copy in to_low()[3:]:
-            copy.wait_recv()
+            for job in pending[:share_of]:
+                contract(*job)
+            pending = pending[share_of:]
+        pending = jobs(chunk, 0, inner)
 
     for copy in to_sides():
         copy.wait_recv()
@@ -481,9 +422,8 @@
     group = strip_lane // (2 * NX)
     is_right = strip_lane % (2 * NX) < NX
     scale = jnp.where(group < 3, 2.0, jnp.where(group < 6, 4.0, 0.0))
-    for start in range(0, all_planes, ROWS):
-        rows = slice(start, start + ROWS)
-        low_rows = slice(all_planes + start, all_planes + start + ROWS)
+
+    def form_strips(rows, into, hi_rows, lo_rows):
         h = upright_height[rows, :]
         from_left = halo_strips[0, rows, :]
         from_right = halo_strips[1, rows, :]
@@ -507,28 +447,109 @@
         for k, y in enumerate((ha, second, third)):
             hi, lo = halves(y)
             at = slice(k * LANES, (k + 1) * LANES)
-            packed_pieces[rows, at] = hi
-            packed_pieces[low_rows, at] = lo
-    mask_all = inside[...].astype(jnp.bfloat16)[:, :all_planes]
-    packed_out[...] = band(jnp.concatenate([mask_all, mask_all], axis=1), packed_pieces[...])
-
-    half = LANES // 2
-    joint = (strip_lane >= half - NX) & (strip_lane < half + NX)
-    tail = slice(LANES, width)
+            into[hi_rows, at] = hi
+            into[lo_rows, at] = lo
+
     for start in range(0, planes, ROWS):
         rows = slice(start, start + ROWS)
+        form_strips(rows, packed_pieces, rows, slice(planes + start, planes + start + ROWS))
+    packed_out[...] = band(mask_own, packed_pieces[...])
+
+    half = LANES // 2
+    edge_lane = lane_index(8)
+    joint = (edge_lane >= half - NX) & (edge_lane < half + NX)
+    tail = slice(LANES, width)
+
+    def add_edges(start):
+        rows = slice(start, start + 8)
         edge = [streamwise4(packed_out[rows, k * LANES : (k + 1) * LANES]) for k in range(3)]
         for f in range(FIELDS):
             t, g = PACKED_AT[f]
             shift = (half - NX - 2 * NX * g) % LANES
             x = pltpu.roll(edge[t], shift, 1) if shift else edge[t]
             filt[chunks - 1, f, rows, tail] = filt[chunks - 1, f, rows, tail] + jnp.where(joint, x, 0.0)
-        contract(chunks - 1, start, tail)
+
+    for job in pending:
+        contract(*job)
+    for start in range(0, inner, 8):
+        add_edges(start)
+        contract(chunks - 1, start, 1)
+
+    def await_halo(which):
+        @pl.when(has_low)
+        def _():
+            for copy in to_high()[which]:
+                copy.wait_recv()
+
+        @pl.when(has_high)
+        def _():
+            for copy in to_low()[which]:
+                copy.wait_recv()
+
+    await_halo(slice(0, 2))
+    heights[1:2, 0:planes] = halo_heights[0]
+    heights[2:3, 0:planes] = halo_heights[1]
+    below_row = pltpu.roll(heights[1:2, :], HMAX, 1)
+    above_row = pltpu.roll(heights[2:3, :], planes + HMAX, 1)
+    lane_row = lax.broadcasted_iota(jnp.int32, (1, LANES), 1)
+    row = jnp.where(
+        lane_row < planes,
+        heights[0:1, :],
+        jnp.where(lane_row < planes + HMAX, below_row, above_row),
+    )
+    heights[0:1, :] = row
+    rim_lane = lax.broadcasted_iota(jnp.int32, (ROWS, LANES), 1)
+    rim_sub = lax.broadcasted_iota(jnp.int32, (ROWS, LANES), 0)
+    upright_height[planes:all_planes, :] = jnp.broadcast_to(
+        upright(0, rim_lane == rim_sub + planes), (ROWS, LANES)
+    )
+    rim_inside = inside[inner:planes, :]
+    rim_weights = rim_inside * row
+    norm[inner:planes, :] = jnp.broadcast_to(
+        (1.0 / 16.0) / jnp.sum(rim_weights, axis=1, keepdims=True), (ROWS, LANES)
+    )
+    rim_mask = jnp.concatenate([rim_inside.astype(jnp.bfloat16)[:, planes:all_planes]] * 2, axis=1)
+    rim_weights = jnp.concatenate(halves(rim_weights[:, planes:all_planes]), axis=1)
+
+    rim_places = (slice(planes, all_planes), halo_pieces, slice(0, ROWS), slice(ROWS, 2 * ROWS))
+
+    def rim_fields(first, stop):
+        for f in range(first, stop):
+            for start in range(0, cells, width):
+                lanes = slice(start, start + width)
+                if 9 <= f < 15:
+                    s = halo_s[f - 9, :, lanes].astype(jnp.bfloat16)
+                    x = band(rim_weights, jnp.concatenate([s, s], axis=0))
+                else:
+                    x = band(rim_mask, halo_pieces[f if f < 9 else f - 6, :, lanes])
+                put(wall_rim, slice(f * ROWS, (f + 1) * ROWS), start, rim[f, :, lanes] + x)
+        for chunk in range(chunks):
+            x = along(wall_rim, slice(first * ROWS, stop * ROWS), chunk)
+            filt[chunk, first:stop, inner:planes] = x.reshape(stop - first, ROWS, width)
+
+    form_flow(lambda c, lanes: halo_u[c, :, lanes], *rim_places)
+    rim_fields(0, 9)
+
+    await_halo(slice(2, 3))
+    form_rates(lambda c, lanes: halo_s[c, :, lanes], *rim_places)
+    rim_fields(9, FIELDS)
+    for chunk in range(chunks):
+        for job in jobs(chunk, inner, planes):
+            contract(*job)
+
+    await_halo(slice(3, 5))
+    form_strips(
+        slice(planes, all_planes), rim_packed, slice(0, ROWS), slice(ROWS, 2 * ROWS)
+    )
+    packed_out[inner:planes, :] = packed_out[inner:planes, :] + band(rim_mask, rim_packed[...])
+    for start in range(inner, planes, 8):
+        add_edges(start)
+        contract(chunks - 1, start, 1)
 
     q = norm[...]
     scaled = jnp.concatenate([acc[:, 0:LANES] * (q * q), acc[:, LANES:width] * (q * q)], axis=1)
-    pick_row = lax.broadcasted_iota(jnp.int32, (8, 2 * LANES), 0)
-    pick_lane = lax.broadcasted_iota(jnp.int32, (8, 2 * LANES), 1)
+    pick_row = lax.broadcasted_iota(jnp.int32, (2, 2 * LANES), 0)
+    pick_lane = lax.broadcasted_iota(jnp.int32, (2, 2 * LANES), 1)
     pick = jnp.where(pick_row == pick_lane // LANES, 1.0, 0.0)
     part[...] = jnp.zeros_like(part)
     part[:, 0:planes] = lax.dot_general(
@@ -556,7 +577,7 @@
     for step in range(1, n_z):
         source = lax.rem(mz + n_z - step, n_z)
         share(step, source, source, step).wait_recv()
-    total = jnp.zeros((8, LANES), jnp.float32)
+    total = jnp.zeros((2, LANES), jnp.float32)
     for k in range(n_z):
         total = total + slots[k]
     count = 1.0 * n_z * cells
@@ -611,12 +632,12 @@
             pltpu.VMEM((FIELDS, ROWS, cells), f32),
             pltpu.VMEM((6 * LANES, 2 * LANES), bf16),
             pltpu.VMEM((6 * LANES, 2 * LANES), bf16),
-            pltpu.VMEM((2 * all_planes, 3 * LANES), bf16),
+            pltpu.VMEM((2 * planes, 3 * LANES), bf16),
+            pltpu.VMEM((2 * ROWS, 3 * LANES), bf16),
             pltpu.VMEM((planes, 3 * LANES), f32),
             pltpu.VMEM((cells // (2 * LANES), FIELDS, planes, 2 * LANES), f32),
             pltpu.VMEM((3, 2 * HMAX, cells), f32),
             pltpu.VMEM((6, 2 * HMAX, cells), f32),
-            pltpu.VMEM((6, 2 * HMAX, cells), bf16),
             pltpu.VMEM((2, 6, HMAX, cells), f32),
             pltpu.VMEM((2, planes, LANES), f32),
             pltpu.VMEM((2, all_planes, LANES), f32),
@@ -625,8 +646,8 @@
             pltpu.VMEM((all_planes, LANES), f32),
             pltpu.VMEM((planes, LANES), f32),
             pltpu.VMEM((planes, 2 * LANES), f32),
-            pltpu.VMEM((8, LANES), f32),
-            pltpu.VMEM((n_z, 8, LANES), f32),
+            pltpu.VMEM((2, LANES), f32),
+            pltpu.VMEM((n_z, 2, LANES), f32),
             pltpu.SemaphoreType.DMA((12,)),
             pltpu.SemaphoreType.DMA((12,)),
             pltpu.SemaphoreType.DMA((n_z,)),

time: 19.2 us -> 20.2 us (1.052)
  Pallas kernels: 17.9 us -> 18.9 us
    pallas_call x1, Pallas kernels: 17.9 us -> 18.9 us  [local(): pl.pallas_call(functools.partial(kernel, n_y, n_z), out_shape=jax.ShapeDt...]
where the time goes in v3:
time: 20.2 us; the launch traced here: 20 us
  Pallas kernels  18.9 us (94%)
  local copies, waits for them, and re-layouts  1.1 us (5%)
    pallas_call x1, Pallas kernels, local(): pl.pallas_call(functools.partial(kernel, n_y, n_z), out_shape=jax.ShapeDt...  18.9 us
    unnamed x3, local copies, waits for them, and re-layouts  1.1 us

profile of v3, /device:TPU:0, one launch (start us, length us, event | category | flops | bytes accessed | tf_op | source)
XLA Modules:
  0.0 20.0 jit_solution(3111225467716307779)
XLA Ops:
  0.0 18.9 %shard_map.46 = f32[1,96]{1,0:T(1,128)} custom-call(f32[3,96,768]{2,1,0:T(8,128)} %vel_hbm.1, bf16[6,96,768]{2,1,0:T(8,128)(2,1)} %strain_hbm.1, f32[1,96]{1,0:T(1,128)} %bitcast.2, s32[2,96]{1,0:T(2,128)} %reach_hbm.1), custom_call_target="tpu_custom_call" | custom-call | tf_op jit(solution)/shard_map/pallas_call | solution.py:618
  18.9 0.0 copy-start
  18.9 0.6 %copy-done = f32[1,96]{1,0:T(1,128)S(1)} copy-done((f32[1,96]{1,0:T(1,128)S(1)}, f32[1,96]{1,0:T(1,128)}, u32[]{:S(2)}) %copy-start) | copy-done | bytes 408
  19.5 0.5 %copy.6 = f32[96]{0:T(128)} copy(f32[96]{0:T(128)S(1)} %bitcast.3) | data formatting | bytes 768
Async XLA Ops:
  18.9 0.6 %copy-start = (f32[1,96]{1,0:T(1,128)S(1)}, f32[1,96]{1,0:T(1,128)}, u32[]{:S(2)}) copy-start(f32[1,96]{1,0:T(1,128)} %shard_map.46) | copy-start | bytes 1156

commit v4 on v3

--- a/solution.py
+++ b/solution.py
@@ -106,6 +106,7 @@
     part_send,
     part_recv,
     load_sem,
+    known,
     inside,
 ):
     planes, cells = vel.shape[1], vel.shape[2]
@@ -139,18 +140,10 @@
     def greet(device):
         pl.semaphore_signal(barrier, inc=1, device_id=device, device_id_type=MESH)
 
-    for step in range(1, n_z):
-        greet({"gy": my, "gz": lax.rem(mz + step, n_z)})
-
-    @pl.when(has_low)
-    def _():
-        for z in (mz, left, right):
-            greet({"gy": low, "gz": z})
-
-    @pl.when(has_high)
-    def _():
-        for z in (mz, left, right):
-            greet({"gy": high, "gz": z})
+    greet({"gy": my, "gz": left})
+    greet({"gy": my, "gz": right})
+    pl.when(has_low)(lambda: greet({"gy": low, "gz": mz}))
+    pl.when(has_high)(lambda: greet({"gy": high, "gz": mz}))
 
     horizontal(window, False)
     horizontal(window_parted, True)
@@ -260,16 +253,19 @@
         form_flow(lambda c, lanes: vel[c, rows, lanes], *places)
         return carry
 
-    blocks = planes // ROWS
-    early = blocks - blocks // 3
-    lax.fori_loop(0, early, own_block, 0)
-
-    partners = (
-        (n_z - 1)
-        + 3 * has_low.astype(jnp.int32)
-        + 3 * has_high.astype(jnp.int32)
-    )
+    partners = 2 + has_low.astype(jnp.int32) + has_high.astype(jnp.int32)
     pl.semaphore_wait(barrier, partners)
+
+    def tell(r):
+        for z in (lax.rem(mz + 2**r, n_z), lax.rem(mz + n_z - 2**r, n_z)):
+            pl.semaphore_signal(
+                known.at[r], inc=1, device_id={"gy": my, "gz": z}, device_id_type=MESH
+            )
+
+    def hear(r):
+        pl.semaphore_wait(known.at[r], 2)
+
+    rounds = max((n_z // 2 - 1).bit_length(), 0)
 
     def remote(src, dst, index, device):
         return pltpu.make_async_remote_copy(
@@ -291,8 +287,8 @@
             remote(height, halo_heights.at[0], 2, here),
             remote(vel_hbm.at[:, top, :], halo_u.at[:, 0:HMAX, :], 0, here),
             remote(send_s.at[1], halo_s.at[:, 0:HMAX, :], 1, here),
-            remote(strips.at[0, top, :], halo_strips.at[1, under, :], 3, {"gy": high, "gz": left}),
-            remote(strips.at[1, top, :], halo_strips.at[0, under, :], 4, {"gy": high, "gz": right}),
+            remote(halo_strips.at[0, top, :], halo_strips.at[0, under, :], 3, here),
+            remote(halo_strips.at[1, top, :], halo_strips.at[1, under, :], 4, here),
         ]
 
     def to_low():
@@ -301,8 +297,8 @@
             remote(height, halo_heights.at[1], 7, here),
             remote(vel_hbm.at[:, 0:HMAX, :], halo_u.at[:, HMAX : 2 * HMAX, :], 5, here),
             remote(send_s.at[0], halo_s.at[:, HMAX : 2 * HMAX, :], 6, here),
-            remote(strips.at[0, 0:HMAX, :], halo_strips.at[1, over, :], 8, {"gy": low, "gz": left}),
-            remote(strips.at[1, 0:HMAX, :], halo_strips.at[0, over, :], 9, {"gy": low, "gz": right}),
+            remote(halo_strips.at[0, 0:HMAX, :], halo_strips.at[0, over, :], 8, here),
+            remote(halo_strips.at[1, 0:HMAX, :], halo_strips.at[1, over, :], 9, here),
         ]
 
     def to_sides():
@@ -311,18 +307,22 @@
             remote(strips.at[1], halo_strips.at[0, 0:planes, :], 11, {"gy": my, "gz": right}),
         ]
 
-    @pl.when(has_high)
-    def _():
-        for copy in to_high():
-            copy.start()
-
-    @pl.when(has_low)
-    def _():
-        for copy in to_low():
-            copy.start()
-
+    def send_halo(which):
+        @pl.when(has_high)
+        def _():
+            for copy in to_high()[which]:
+                copy.start()
+
+        @pl.when(has_low)
+        def _():
+            for copy in to_low()[which]:
+                copy.start()
+
+    send_halo(slice(0, 3))
     for copy in to_sides():
         copy.start()
+    if rounds:
+        tell(0)
 
     def clear(side):
         span = slice(side * HMAX, (side + 1) * HMAX)
@@ -335,7 +335,7 @@
     pl.when(jnp.logical_not(has_low))(lambda: clear(0))
     pl.when(jnp.logical_not(has_high))(lambda: clear(1))
 
-    lax.fori_loop(early, blocks, own_block, 0)
+    lax.fori_loop(0, planes // ROWS, own_block, 0)
 
     acc[...] = jnp.zeros_like(acc)
     width = 2 * LANES
@@ -359,6 +359,10 @@
                 x = band(mask_own, pieces[f if f < 9 else f - 6, :, lanes])
             put(wall, slice(f * inner, (f + 1) * inner), start, x[:inner])
             rim[f, :, lanes] = x[inner:]
+
+    for r in range(1, rounds):
+        hear(r - 1)
+        tell(r)
 
     def along(ref, rows, chunk):
         last = chunk == chunks - 1
@@ -406,6 +410,10 @@
     step_fields = 3
     pending = []
     for chunk in range(chunks):
+        if chunk == chunks - 1:
+            for copy in to_sides():
+                copy.wait_recv()
+            send_halo(slice(3, 5))
         share_of = -(-len(pending) // (FIELDS // step_fields))
         for f in range(0, FIELDS, step_fields):
             x = along(wall, slice(f * inner, (f + step_fields) * inner), chunk)
@@ -414,9 +422,6 @@
                 contract(*job)
             pending = pending[share_of:]
         pending = jobs(chunk, 0, inner)
-
-    for copy in to_sides():
-        copy.wait_recv()
 
     strip_lane = lane_index(ROWS)
     group = strip_lane // (2 * NX)
@@ -571,6 +576,8 @@
             device_id_type=MESH,
         )
 
+    if rounds:
+        hear(rounds - 1)
     for step in range(1, n_z):
         peer = lax.rem(mz + step, n_z)
         share(step, peer, mz, step).start()
@@ -653,6 +660,7 @@
             pltpu.SemaphoreType.DMA((n_z,)),
             pltpu.SemaphoreType.DMA((n_z,)),
             pltpu.SemaphoreType.DMA((6,)),
+            pltpu.SemaphoreType.REGULAR((max((n_z // 2 - 1).bit_length(), 1),)),
             pltpu.VMEM((planes, LANES), f32),
         ],
         compiler_params=pltpu.CompilerParams(

time: 20.2 us -> 20.2 us (level)
  no operation moved by 1% of the time
where the time goes in v4:
time: 20.2 us; the launch traced here: 20 us
  Pallas kernels  18.9 us (94%)
  local copies, waits for them, and re-layouts  1.1 us (5%)
    pallas_call x1, Pallas kernels, local(): pl.pallas_call(functools.partial(kernel, n_y, n_z), out_shape=jax.ShapeDt...  18.9 us
    unnamed x3, local copies, waits for them, and re-layouts  1.1 us

profile of v4, /device:TPU:0, one launch (start us, length us, event | category | flops | bytes accessed | tf_op | source)
XLA Modules:
  0.0 20.0 jit_solution(6303608298366664927)
XLA Ops:
  0.0 18.9 %shard_map.46 = f32[1,96]{1,0:T(1,128)} custom-call(f32[3,96,768]{2,1,0:T(8,128)} %vel_hbm.1, bf16[6,96,768]{2,1,0:T(8,128)(2,1)} %strain_hbm.1, f32[1,96]{1,0:T(1,128)} %bitcast.2, s32[2,96]{1,0:T(2,128)} %reach_hbm.1), custom_call_target="tpu_custom_call" | custom-call | tf_op jit(solution)/shard_map/pallas_call | solution.py:625
  18.9 0.0 copy-start
  18.9 0.6 %copy-done = f32[1,96]{1,0:T(1,128)S(1)} copy-done((f32[1,96]{1,0:T(1,128)S(1)}, f32[1,96]{1,0:T(1,128)}, u32[]{:S(2)}) %copy-start) | copy-done | bytes 408
  19.5 0.5 %copy.6 = f32[96]{0:T(128)} copy(f32[96]{0:T(128)S(1)} %bitcast.3) | data formatting | bytes 768
Async XLA Ops:
  18.9 0.6 %copy-start = (f32[1,96]{1,0:T(1,128)S(1)}, f32[1,96]{1,0:T(1,128)}, u32[]{:S(2)}) copy-start(f32[1,96]{1,0:T(1,128)} %shard_map.46) | copy-start | bytes 1156

commit v5 on v4

--- a/solution.py
+++ b/solution.py
@@ -112,19 +112,26 @@
     planes, cells = vel.shape[1], vel.shape[2]
     all_planes = planes + 2 * HMAX
     inner = planes - 2 * HMAX
-    bottom = slice(0, ROWS)
-    middle = slice(ROWS, planes - ROWS)
+    ends = 2 * ROWS
+    bottom = slice(0, ends)
+    middle = slice(ends, planes - ROWS)
     summit = slice(planes - ROWS, planes)
+
+    def load(src, dst, at):
+        return pltpu.make_async_copy(src, dst, load_sem.at[at])
+
     loads = [
-        pltpu.make_async_copy(height_hbm, height, load_sem.at[0]),
-        pltpu.make_async_copy(reach_hbm, reach, load_sem.at[1]),
-        pltpu.make_async_copy(strain_hbm.at[:, bottom, :], strain.at[:, bottom, :], load_sem.at[2]),
-        pltpu.make_async_copy(strain_hbm.at[:, summit, :], strain.at[:, summit, :], load_sem.at[3]),
-        pltpu.make_async_copy(vel_hbm, vel, load_sem.at[4]),
-        pltpu.make_async_copy(strain_hbm.at[:, middle, :], strain.at[:, middle, :], load_sem.at[5]),
+        load(height_hbm, height, 0),
+        load(reach_hbm, reach, 1),
+        load(strain_hbm.at[:, bottom, :], strain.at[:, bottom, :], 2),
+        load(strain_hbm.at[:, summit, :], strain.at[:, summit, :], 3),
+        load(vel_hbm.at[:, bottom, :], vel.at[:, bottom, :], 4),
+        load(strain_hbm.at[:, middle, :], strain.at[:, middle, :], 5),
+        load(vel_hbm.at[:, middle, :], vel.at[:, middle, :], 6),
+        load(vel_hbm.at[:, summit, :], vel.at[:, summit, :], 7),
     ]
-    for load in loads:
-        load.start()
+    for copy in loads:
+        copy.start()
     tiles = cells // LANES
     my = lax.axis_index("gy")
     mz = lax.axis_index("gz")
@@ -148,8 +155,8 @@
     horizontal(window, False)
     horizontal(window_parted, True)
 
-    for load in loads[:4]:
-        load.wait()
+    for copy in loads[:4]:
+        copy.wait()
     for c in range(6):
         send_s[0, c] = strain[c, 0:ROWS, :].astype(jnp.float32)[0:HMAX]
         send_s[1, c] = strain[c, planes - ROWS : planes, :].astype(jnp.float32)[HMAX:ROWS]
@@ -186,9 +193,6 @@
     mask_own = jnp.concatenate([mask[:, :planes]] * 2, axis=1)
     weights_own = jnp.concatenate(halves(weights[:, :planes]), axis=1)
 
-    for load in loads[4:]:
-        load.wait()
-
     def pack(i, carry):
         rows = pl.ds(pl.multiple_of(i * ROWS, ROWS), ROWS)
         lane = lane_index(ROWS)
@@ -213,7 +217,6 @@
         strips[1, rows, :] = last
         return carry
 
-    lax.fori_loop(0, planes // ROWS, pack, 0)
 
     def emit_to(into, hi_rows, lo_rows, lanes):
         def emit(f, x):
@@ -253,6 +256,12 @@
         form_flow(lambda c, lanes: vel[c, rows, lanes], *places)
         return carry
 
+    loads[4].wait()
+    lax.fori_loop(0, ends // ROWS, own_block, 0)
+    for copy in loads[5:]:
+        copy.wait()
+    lax.fori_loop(0, planes // ROWS, pack, 0)
+
     partners = 2 + has_low.astype(jnp.int32) + has_high.astype(jnp.int32)
     pl.semaphore_wait(barrier, partners)
 
@@ -287,8 +296,8 @@
             remote(height, halo_heights.at[0], 2, here),
             remote(vel_hbm.at[:, top, :], halo_u.at[:, 0:HMAX, :], 0, here),
             remote(send_s.at[1], halo_s.at[:, 0:HMAX, :], 1, here),
-            remote(halo_strips.at[0, top, :], halo_strips.at[0, under, :], 3, here),
-            remote(halo_strips.at[1, top, :], halo_strips.at[1, under, :], 4, here),
+            remote(strips.at[0, top, :], halo_strips.at[1, under, :], 3, {"gy": high, "gz": left}),
+            remote(strips.at[1, top, :], halo_strips.at[0, under, :], 4, {"gy": high, "gz": right}),
         ]
 
     def to_low():
@@ -297,8 +306,8 @@
             remote(height, halo_heights.at[1], 7, here),
             remote(vel_hbm.at[:, 0:HMAX, :], halo_u.at[:, HMAX : 2 * HMAX, :], 5, here),
             remote(send_s.at[0], halo_s.at[:, HMAX : 2 * HMAX, :], 6, here),
-            remote(halo_strips.at[0, 0:HMAX, :], halo_strips.at[0, over, :], 8, here),
-            remote(halo_strips.at[1, 0:HMAX, :], halo_strips.at[1, over, :], 9, here),
+            remote(strips.at[0, 0:HMAX, :], halo_strips.at[1, over, :], 8, {"gy": low, "gz": left}),
+            remote(strips.at[1, 0:HMAX, :], halo_strips.at[0, over, :], 9, {"gy": low, "gz": right}),
         ]
 
     def to_sides():
@@ -335,7 +344,7 @@
     pl.when(jnp.logical_not(has_low))(lambda: clear(0))
     pl.when(jnp.logical_not(has_high))(lambda: clear(1))
 
-    lax.fori_loop(0, planes // ROWS, own_block, 0)
+    lax.fori_loop(ends // ROWS, planes // ROWS, own_block, 0)
 
     acc[...] = jnp.zeros_like(acc)
     width = 2 * LANES
@@ -360,6 +369,19 @@
             put(wall, slice(f * inner, (f + 1) * inner), start, x[:inner])
             rim[f, :, lanes] = x[inner:]
 
+    def await_halo(which):
+        @pl.when(has_low)
+        def _():
+            for copy in to_high()[which]:
+                copy.wait_recv()
+
+        @pl.when(has_high)
+        def _():
+            for copy in to_low()[which]:
+                copy.wait_recv()
+
+    await_halo(slice(0, 1))
+    send_halo(slice(3, 5))
     for r in range(1, rounds):
         hear(r - 1)
         tell(r)
@@ -410,10 +432,6 @@
     step_fields = 3
     pending = []
     for chunk in range(chunks):
-        if chunk == chunks - 1:
-            for copy in to_sides():
-                copy.wait_recv()
-            send_halo(slice(3, 5))
         share_of = -(-len(pending) // (FIELDS // step_fields))
         for f in range(0, FIELDS, step_fields):
             x = along(wall, slice(f * inner, (f + step_fields) * inner), chunk)
@@ -422,6 +440,12 @@
                 contract(*job)
             pending = pending[share_of:]
         pending = jobs(chunk, 0, inner)
+    for job in pending:
+        contract(*job)
+
+    for copy in to_sides():
+        copy.wait_recv()
+    await_halo(slice(1, 3))
 
     strip_lane = lane_index(ROWS)
     group = strip_lane // (2 * NX)
@@ -474,24 +498,6 @@
             x = pltpu.roll(edge[t], shift, 1) if shift else edge[t]
             filt[chunks - 1, f, rows, tail] = filt[chunks - 1, f, rows, tail] + jnp.where(joint, x, 0.0)
 
-    for job in pending:
-        contract(*job)
-    for start in range(0, inner, 8):
-        add_edges(start)
-        contract(chunks - 1, start, 1)
-
-    def await_halo(which):
-        @pl.when(has_low)
-        def _():
-            for copy in to_high()[which]:
-                copy.wait_recv()
-
-        @pl.when(has_high)
-        def _():
-            for copy in to_low()[which]:
-                copy.wait_recv()
-
-    await_halo(slice(0, 2))
     heights[1:2, 0:planes] = halo_heights[0]
     heights[2:3, 0:planes] = halo_heights[1]
     below_row = pltpu.roll(heights[1:2, :], HMAX, 1)
@@ -533,11 +539,11 @@
             filt[chunk, first:stop, inner:planes] = x.reshape(stop - first, ROWS, width)
 
     form_flow(lambda c, lanes: halo_u[c, :, lanes], *rim_places)
-    rim_fields(0, 9)
-
-    await_halo(slice(2, 3))
     form_rates(lambda c, lanes: halo_s[c, :, lanes], *rim_places)
-    rim_fields(9, FIELDS)
+    rim_fields(0, FIELDS)
+    for start in range(0, inner, 8):
+        add_edges(start)
+        contract(chunks - 1, start, 1)
     for chunk in range(chunks):
         for job in jobs(chunk, inner, planes):
             contract(*job)
@@ -659,12 +665,12 @@
             pltpu.SemaphoreType.DMA((12,)),
             pltpu.SemaphoreType.DMA((n_z,)),
             pltpu.SemaphoreType.DMA((n_z,)),
-            pltpu.SemaphoreType.DMA((6,)),
+            pltpu.SemaphoreType.DMA((8,)),
             pltpu.SemaphoreType.REGULAR((max((n_z // 2 - 1).bit_length(), 1),)),
             pltpu.VMEM((planes, LANES), f32),
         ],
         compiler_params=pltpu.CompilerParams(
-            collective_id=0, has_side_effects=True, vmem_limit_bytes=67043328
+            collective_id=0, has_side_effects=True, vmem_limit_bytes=67043328 - 10490000
         ),
     )(velocity, strain, cell_height.reshape(1, planes), stencil_reach)
     return result.reshape(planes)

time: 20.2 us -> 18.4 us (0.911)
  Pallas kernels: 18.9 us -> 17.8 us
  local copies, waits for them, and re-layouts: 1.1 us -> 0.51 us
    pallas_call x1, Pallas kernels: 18.9 us -> 17.8 us  [local(): pl.pallas_call(functools.partial(kernel, n_y, n_z), out_shape=jax.ShapeDt...]
    unnamed x3 -> x1, local copies, waits for them, and re-layouts: 1.1 us -> 0.51 us
where the time goes in v5:
time: 18.4 us; the launch traced here: 18.3 us
  Pallas kernels  17.8 us (97%)
  local copies, waits for them, and re-layouts  0.51 us (3%)
    pallas_call x1, Pallas kernels, local(): pl.pallas_call(functools.partial(kernel, n_y, n_z), out_shape=jax.ShapeDt...  17.8 us
    unnamed x1, local copies, waits for them, and re-layouts  0.51 us

profile of v5, /device:TPU:0, one launch (start us, length us, event | category | flops | bytes accessed | tf_op | source)
XLA Modules:
  0.0 18.3 jit_solution(5104528882038843977)
XLA Ops:
  0.0 17.8 %shard_map.46 = f32[1,96]{1,0:T(1,128)S(1)} custom-call(f32[3,96,768]{2,1,0:T(8,128)} %vel_hbm.1, bf16[6,96,768]{2,1,0:T(8,128)(2,1)} %strain_hbm.1, f32[1,96]{1,0:T(1,128)} %bitcast.3, s32[2,96]{1,0:T(2,128)} %reach_hbm.1), custom_call_target="tpu_custom_call" | custom-call | tf_op jit(solution)/shard_map/pallas_call | solution.py:631
  17.8 0.5 %copy.6 = f32[96]{0:T(128)} copy(f32[96]{0:T(128)S(1)} %bitcast.2) | data formatting | bytes 768

commit v6 on v5

--- a/solution.py
+++ b/solution.py
@@ -107,6 +107,7 @@
     part_recv,
     load_sem,
     known,
+    passed,
     inside,
 ):
     planes, cells = vel.shape[1], vel.shape[2]
@@ -333,6 +334,14 @@
     if rounds:
         tell(0)
 
+    def notify(y):
+        pl.semaphore_signal(
+            passed, inc=1, device_id={"gy": y, "gz": mz}, device_id_type=MESH
+        )
+
+    pl.when(has_low)(lambda: notify(low))
+    pl.when(has_high)(lambda: notify(high))
+
     def clear(side):
         span = slice(side * HMAX, (side + 1) * HMAX)
         halo_u[:, span, :] = jnp.zeros((3, HMAX, cells), jnp.float32)
@@ -345,6 +354,9 @@
     pl.when(jnp.logical_not(has_high))(lambda: clear(1))
 
     lax.fori_loop(ends // ROWS, planes // ROWS, own_block, 0)
+
+    pl.semaphore_wait(passed, has_low.astype(jnp.int32) + has_high.astype(jnp.int32))
+    send_halo(slice(3, 5))
 
     acc[...] = jnp.zeros_like(acc)
     width = 2 * LANES
@@ -379,12 +391,6 @@
         def _():
             for copy in to_low()[which]:
                 copy.wait_recv()
-
-    await_halo(slice(0, 1))
-    send_halo(slice(3, 5))
-    for r in range(1, rounds):
-        hear(r - 1)
-        tell(r)
 
     def along(ref, rows, chunk):
         last = chunk == chunks - 1
@@ -443,9 +449,12 @@
     for job in pending:
         contract(*job)
 
+    for r in range(1, rounds):
+        hear(r - 1)
+        tell(r)
     for copy in to_sides():
         copy.wait_recv()
-    await_halo(slice(1, 3))
+    await_halo(slice(0, 3))
 
     strip_lane = lane_index(ROWS)
     group = strip_lane // (2 * NX)
@@ -667,6 +676,7 @@
             pltpu.SemaphoreType.DMA((n_z,)),
             pltpu.SemaphoreType.DMA((8,)),
             pltpu.SemaphoreType.REGULAR((max((n_z // 2 - 1).bit_length(), 1),)),
+            pltpu.SemaphoreType.REGULAR,
             pltpu.VMEM((planes, LANES), f32),
         ],
         compiler_params=pltpu.CompilerParams(

time: 18.4 us -> 17.7 us (0.962)
  Pallas kernels: 17.8 us -> 17 us
    pallas_call x1, Pallas kernels: 17.8 us -> 17 us  [local(): pl.pallas_call(functools.partial(kernel, n_y, n_z), out_shape=jax.ShapeDt...]
where the time goes in v6:
time: 17.7 us; the launch traced here: 17.5 us
  Pallas kernels  17 us (96%)
  local copies, waits for them, and re-layouts  0.51 us (3%)
    pallas_call x1, Pallas kernels, local(): pl.pallas_call(functools.partial(kernel, n_y, n_z), out_shape=jax.ShapeDt...  17 us
    unnamed x1, local copies, waits for them, and re-layouts  0.51 us

profile of v6, /device:TPU:0, one launch (start us, length us, event | category | flops | bytes accessed | tf_op | source)
XLA Modules:
  0.0 17.5 jit_solution(227442874749057489)
XLA Ops:
  0.0 17.0 %shard_map.46 = f32[1,96]{1,0:T(1,128)S(1)} custom-call(f32[3,96,768]{2,1,0:T(8,128)} %vel_hbm.1, bf16[6,96,768]{2,1,0:T(8,128)(2,1)} %strain_hbm.1, f32[1,96]{1,0:T(1,128)} %bitcast.3, s32[2,96]{1,0:T(2,128)} %reach_hbm.1), custom_call_target="tpu_custom_call" | custom-call | tf_op jit(solution)/shard_map/pallas_call | solution.py:640
  17.0 0.5 %copy.6 = f32[96]{0:T(128)} copy(f32[96]{0:T(128)S(1)} %bitcast.2) | data formatting | bytes 768

commit v7 on v6

--- a/solution.py
+++ b/solution.py
@@ -113,24 +113,34 @@
     planes, cells = vel.shape[1], vel.shape[2]
     all_planes = planes + 2 * HMAX
     inner = planes - 2 * HMAX
-    ends = 2 * ROWS
-    bottom = slice(0, ends)
-    middle = slice(ends, planes - ROWS)
+    bottom = slice(0, ROWS)
+    middle = slice(ROWS, planes - ROWS)
     summit = slice(planes - ROWS, planes)
-
-    def load(src, dst, at):
-        return pltpu.make_async_copy(src, dst, load_sem.at[at])
-
+    whole = slice(0, planes)
+    first_tile = slice(0, LANES)
+    last_tile = slice(cells - LANES, cells)
+    between = slice(LANES, cells - LANES)
     loads = [
-        load(height_hbm, height, 0),
-        load(reach_hbm, reach, 1),
-        load(strain_hbm.at[:, bottom, :], strain.at[:, bottom, :], 2),
-        load(strain_hbm.at[:, summit, :], strain.at[:, summit, :], 3),
-        load(vel_hbm.at[:, bottom, :], vel.at[:, bottom, :], 4),
-        load(strain_hbm.at[:, middle, :], strain.at[:, middle, :], 5),
-        load(vel_hbm.at[:, middle, :], vel.at[:, middle, :], 6),
-        load(vel_hbm.at[:, summit, :], vel.at[:, summit, :], 7),
+        pltpu.make_async_copy(src.at[:, rows, lanes], dst.at[:, rows, lanes], load_sem.at[k])
+        for k, (src, dst, rows, lanes) in enumerate(
+            [
+                (strain_hbm, strain, whole, first_tile),
+                (strain_hbm, strain, whole, last_tile),
+                (vel_hbm, vel, whole, first_tile),
+                (vel_hbm, vel, whole, last_tile),
+                (strain_hbm, strain, bottom, between),
+                (strain_hbm, strain, summit, between),
+                (strain_hbm, strain, middle, between),
+                (vel_hbm, vel, whole, between),
+            ]
+        )
     ]
+    tables = [
+        pltpu.make_async_copy(height_hbm, height, load_sem.at[8]),
+        pltpu.make_async_copy(reach_hbm, reach, load_sem.at[9]),
+    ]
+    for copy in tables:
+        copy.start()
     for copy in loads:
         copy.start()
     tiles = cells // LANES
@@ -156,11 +166,170 @@
     horizontal(window, False)
     horizontal(window_parted, True)
 
+    def pack(i, carry):
+        rows = pl.ds(pl.multiple_of(i * ROWS, ROWS), ROWS)
+        lane = lane_index(ROWS)
+        first = jnp.zeros((ROWS, LANES), jnp.float32)
+        last = first
+        for g in range(9):
+            def tile(start):
+                if g < 6:
+                    return strain[g, rows, start : start + LANES].astype(jnp.float32)
+                return vel[g - 6, rows, start : start + LANES]
+
+            a = tile(0)
+            b = tile(cells - LANES)
+            to_first = 2 * g * NX if g < 8 else NX
+            to_last = (2 * g + 1) * NX if g < 8 else 0
+            a = pltpu.roll(a, to_first, 1) if to_first else a
+            move = (to_last + NX) % LANES
+            b = pltpu.roll(b, move, 1) if move else b
+            first = jnp.where((lane >= to_first) & (lane < to_first + NX), a, first)
+            last = jnp.where((lane >= to_last) & (lane < to_last + NX), b, last)
+        strips[0, rows, :] = first
+        strips[1, rows, :] = last
+        return carry
+
+
+    def emit_to(into, hi_rows, lo_rows, lanes):
+        def emit(f, x):
+            hi, lo = halves(x)
+            into[f, hi_rows, lanes] = hi
+            into[f, lo_rows, lanes] = lo
+
+        return emit
+
+    def form_rates(load_s, height_rows, into, hi_rows, lo_rows):
+        h = upright_height[height_rows, :]
+        for t in range(tiles):
+            lanes = slice(t * LANES, (t + 1) * LANES)
+            emit = emit_to(into, hi_rows, lo_rows, lanes)
+            s = [load_s(c, lanes) for c in range(6)]
+            rate = h * strain_rate(s)
+            for c in range(6):
+                emit(9 + c, rate * s[c])
+
+    def form_flow(load_u, height_rows, into, hi_rows, lo_rows):
+        h = upright_height[height_rows, :]
+        for t in range(tiles):
+            lanes = slice(t * LANES, (t + 1) * LANES)
+            emit = emit_to(into, hi_rows, lo_rows, lanes)
+            u = [load_u(c, lanes) for c in range(3)]
+            hu = [h * x for x in u]
+            for c in range(3):
+                emit(c, hu[c])
+            for k in range(6):
+                emit(3 + k, hu[LEAD_INDEX[k]] * u[TAIL_INDEX[k]])
+
+    def own_block(i, carry):
+        start = pl.multiple_of(i * ROWS, ROWS)
+        rows = pl.ds(start, ROWS)
+        places = (rows, pieces, rows, pl.ds(start + planes, ROWS))
+        form_rates(lambda c, lanes: strain[c, rows, lanes].astype(jnp.float32), *places)
+        form_flow(lambda c, lanes: vel[c, rows, lanes], *places)
+        return carry
+
     for copy in loads[:4]:
+        copy.wait()
+    lax.fori_loop(0, planes // ROWS, pack, 0)
+    for copy in loads[4:6]:
         copy.wait()
     for c in range(6):
         send_s[0, c] = strain[c, 0:ROWS, :].astype(jnp.float32)[0:HMAX]
         send_s[1, c] = strain[c, planes - ROWS : planes, :].astype(jnp.float32)[HMAX:ROWS]
+
+    for copy in tables:
+        copy.wait()
+
+    partners = 2 + has_low.astype(jnp.int32) + has_high.astype(jnp.int32)
+    pl.semaphore_wait(barrier, partners)
+
+    def tell(r):
+        for z in (lax.rem(mz + 2**r, n_z), lax.rem(mz + n_z - 2**r, n_z)):
+            pl.semaphore_signal(
+                known.at[r], inc=1, device_id={"gy": my, "gz": z}, device_id_type=MESH
+            )
+
+    def hear(r):
+        pl.semaphore_wait(known.at[r], 2)
+
+    rounds = max((n_z // 2 - 1).bit_length(), 0)
+
+    def remote(src, dst, index, device):
+        return pltpu.make_async_remote_copy(
+            src_ref=src,
+            dst_ref=dst,
+            send_sem=send_sem.at[index],
+            recv_sem=recv_sem.at[index],
+            device_id=device,
+            device_id_type=MESH,
+        )
+
+    top = slice(planes - HMAX, planes)
+    under = slice(planes, planes + HMAX)
+    over = slice(planes + HMAX, planes + 2 * HMAX)
+
+    def to_high():
+        here = {"gy": high, "gz": mz}
+        return [
+            remote(height, halo_heights.at[0], 2, here),
+            remote(vel_hbm.at[:, top, :], halo_u.at[:, 0:HMAX, :], 0, here),
+            remote(send_s.at[1], halo_s.at[:, 0:HMAX, :], 1, here),
+            remote(strips.at[0, top, :], halo_strips.at[1, under, :], 3, {"gy": high, "gz": left}),
+            remote(strips.at[1, top, :], halo_strips.at[0, under, :], 4, {"gy": high, "gz": right}),
+        ]
+
+    def to_low():
+        here = {"gy": low, "gz": mz}
+        return [
+            remote(height, halo_heights.at[1], 7, here),
+            remote(vel_hbm.at[:, 0:HMAX, :], halo_u.at[:, HMAX : 2 * HMAX, :], 5, here),
+            remote(send_s.at[0], halo_s.at[:, HMAX : 2 * HMAX, :], 6, here),
+            remote(strips.at[0, 0:HMAX, :], halo_strips.at[1, over, :], 8, {"gy": low, "gz": left}),
+            remote(strips.at[1, 0:HMAX, :], halo_strips.at[0, over, :], 9, {"gy": low, "gz": right}),
+        ]
+
+    def to_sides():
+        return [
+            remote(strips.at[0], halo_strips.at[1, 0:planes, :], 10, {"gy": my, "gz": left}),
+            remote(strips.at[1], halo_strips.at[0, 0:planes, :], 11, {"gy": my, "gz": right}),
+        ]
+
+    def send_halo(which):
+        @pl.when(has_high)
+        def _():
+            for copy in to_high()[which]:
+                copy.start()
+
+        @pl.when(has_low)
+        def _():
+            for copy in to_low()[which]:
+                copy.start()
+
+    send_halo(slice(0, 3))
+    for copy in to_sides():
+        copy.start()
+    if rounds:
+        tell(0)
+
+    def notify(y):
+        pl.semaphore_signal(
+            passed, inc=1, device_id={"gy": y, "gz": mz}, device_id_type=MESH
+        )
+
+    pl.when(has_low)(lambda: notify(low))
+    pl.when(has_high)(lambda: notify(high))
+
+    def clear(side):
+        span = slice(side * HMAX, (side + 1) * HMAX)
+        halo_u[:, span, :] = jnp.zeros((3, HMAX, cells), jnp.float32)
+        halo_s[:, span, :] = jnp.zeros((6, HMAX, cells), jnp.float32)
+        halo_heights[side] = jnp.zeros(halo_heights.shape[1:], jnp.float32)
+        start = planes + side * HMAX
+        halo_strips[:, start : start + HMAX, :] = jnp.zeros((2, HMAX, LANES), jnp.float32)
+
+    pl.when(jnp.logical_not(has_low))(lambda: clear(0))
+    pl.when(jnp.logical_not(has_high))(lambda: clear(1))
 
     heights[...] = jnp.zeros_like(heights)
     heights[0:1, 0:planes] = height[...]
@@ -194,169 +363,14 @@
     mask_own = jnp.concatenate([mask[:, :planes]] * 2, axis=1)
     weights_own = jnp.concatenate(halves(weights[:, :planes]), axis=1)
 
-    def pack(i, carry):
-        rows = pl.ds(pl.multiple_of(i * ROWS, ROWS), ROWS)
-        lane = lane_index(ROWS)
-        first = jnp.zeros((ROWS, LANES), jnp.float32)
-        last = first
-        for g in range(9):
-            def tile(start):
-                if g < 6:
-                    return strain[g, rows, start : start + LANES].astype(jnp.float32)
-                return vel[g - 6, rows, start : start + LANES]
-
-            a = tile(0)
-            b = tile(cells - LANES)
-            to_first = 2 * g * NX if g < 8 else NX
-            to_last = (2 * g + 1) * NX if g < 8 else 0
-            a = pltpu.roll(a, to_first, 1) if to_first else a
-            move = (to_last + NX) % LANES
-            b = pltpu.roll(b, move, 1) if move else b
-            first = jnp.where((lane >= to_first) & (lane < to_first + NX), a, first)
-            last = jnp.where((lane >= to_last) & (lane < to_last + NX), b, last)
-        strips[0, rows, :] = first
-        strips[1, rows, :] = last
-        return carry
-
-
-    def emit_to(into, hi_rows, lo_rows, lanes):
-        def emit(f, x):
-            hi, lo = halves(x)
-            into[f, hi_rows, lanes] = hi
-            into[f, lo_rows, lanes] = lo
-
-        return emit
-
-    def form_rates(load_s, height_rows, into, hi_rows, lo_rows):
-        h = upright_height[height_rows, :]
-        for t in range(tiles):
-            lanes = slice(t * LANES, (t + 1) * LANES)
-            emit = emit_to(into, hi_rows, lo_rows, lanes)
-            s = [load_s(c, lanes) for c in range(6)]
-            rate = h * strain_rate(s)
-            for c in range(6):
-                emit(9 + c, rate * s[c])
-
-    def form_flow(load_u, height_rows, into, hi_rows, lo_rows):
-        h = upright_height[height_rows, :]
-        for t in range(tiles):
-            lanes = slice(t * LANES, (t + 1) * LANES)
-            emit = emit_to(into, hi_rows, lo_rows, lanes)
-            u = [load_u(c, lanes) for c in range(3)]
-            hu = [h * x for x in u]
-            for c in range(3):
-                emit(c, hu[c])
-            for k in range(6):
-                emit(3 + k, hu[LEAD_INDEX[k]] * u[TAIL_INDEX[k]])
-
-    def own_block(i, carry):
-        start = pl.multiple_of(i * ROWS, ROWS)
-        rows = pl.ds(start, ROWS)
-        places = (rows, pieces, rows, pl.ds(start + planes, ROWS))
-        form_rates(lambda c, lanes: strain[c, rows, lanes].astype(jnp.float32), *places)
-        form_flow(lambda c, lanes: vel[c, rows, lanes], *places)
-        return carry
-
-    loads[4].wait()
-    lax.fori_loop(0, ends // ROWS, own_block, 0)
-    for copy in loads[5:]:
+    for copy in loads[6:]:
         copy.wait()
-    lax.fori_loop(0, planes // ROWS, pack, 0)
-
-    partners = 2 + has_low.astype(jnp.int32) + has_high.astype(jnp.int32)
-    pl.semaphore_wait(barrier, partners)
-
-    def tell(r):
-        for z in (lax.rem(mz + 2**r, n_z), lax.rem(mz + n_z - 2**r, n_z)):
-            pl.semaphore_signal(
-                known.at[r], inc=1, device_id={"gy": my, "gz": z}, device_id_type=MESH
-            )
-
-    def hear(r):
-        pl.semaphore_wait(known.at[r], 2)
-
-    rounds = max((n_z // 2 - 1).bit_length(), 0)
-
-    def remote(src, dst, index, device):
-        return pltpu.make_async_remote_copy(
-            src_ref=src,
-            dst_ref=dst,
-            send_sem=send_sem.at[index],
-            recv_sem=recv_sem.at[index],
-            device_id=device,
-            device_id_type=MESH,
-        )
-
-    top = slice(planes - HMAX, planes)
-    under = slice(planes, planes + HMAX)
-    over = slice(planes + HMAX, planes + 2 * HMAX)
-
-    def to_high():
-        here = {"gy": high, "gz": mz}
-        return [
-            remote(height, halo_heights.at[0], 2, here),
-            remote(vel_hbm.at[:, top, :], halo_u.at[:, 0:HMAX, :], 0, here),
-            remote(send_s.at[1], halo_s.at[:, 0:HMAX, :], 1, here),
-            remote(strips.at[0, top, :], halo_strips.at[1, under, :], 3, {"gy": high, "gz": left}),
-            remote(strips.at[1, top, :], halo_strips.at[0, under, :], 4, {"gy": high, "gz": right}),
-        ]
-
-    def to_low():
-        here = {"gy": low, "gz": mz}
-        return [
-            remote(height, halo_heights.at[1], 7, here),
-            remote(vel_hbm.at[:, 0:HMAX, :], halo_u.at[:, HMAX : 2 * HMAX, :], 5, here),
-            remote(send_s.at[0], halo_s.at[:, HMAX : 2 * HMAX, :], 6, here),
-            remote(strips.at[0, 0:HMAX, :], halo_strips.at[1, over, :], 8, {"gy": low, "gz": left}),
-            remote(strips.at[1, 0:HMAX, :], halo_strips.at[0, over, :], 9, {"gy": low, "gz": right}),
-        ]
-
-    def to_sides():
-        return [
-            remote(strips.at[0], halo_strips.at[1, 0:planes, :], 10, {"gy": my, "gz": left}),
-            remote(strips.at[1], halo_strips.at[0, 0:planes, :], 11, {"gy": my, "gz": right}),
-        ]
-
-    def send_halo(which):
-        @pl.when(has_high)
-        def _():
-            for copy in to_high()[which]:
-                copy.start()
-
-        @pl.when(has_low)
-        def _():
-            for copy in to_low()[which]:
-                copy.start()
-
-    send_halo(slice(0, 3))
-    for copy in to_sides():
-        copy.start()
-    if rounds:
-        tell(0)
-
-    def notify(y):
-        pl.semaphore_signal(
-            passed, inc=1, device_id={"gy": y, "gz": mz}, device_id_type=MESH
-        )
-
-    pl.when(has_low)(lambda: notify(low))
-    pl.when(has_high)(lambda: notify(high))
-
-    def clear(side):
-        span = slice(side * HMAX, (side + 1) * HMAX)
-        halo_u[:, span, :] = jnp.zeros((3, HMAX, cells), jnp.float32)
-        halo_s[:, span, :] = jnp.zeros((6, HMAX, cells), jnp.float32)
-        halo_heights[side] = jnp.zeros(halo_heights.shape[1:], jnp.float32)
-        start = planes + side * HMAX
-        halo_strips[:, start : start + HMAX, :] = jnp.zeros((2, HMAX, LANES), jnp.float32)
-
-    pl.when(jnp.logical_not(has_low))(lambda: clear(0))
-    pl.when(jnp.logical_not(has_high))(lambda: clear(1))
-
-    lax.fori_loop(ends // ROWS, planes // ROWS, own_block, 0)
+    blocks = planes // ROWS
+    lax.fori_loop(0, blocks - 2, own_block, 0)
 
     pl.semaphore_wait(passed, has_low.astype(jnp.int32) + has_high.astype(jnp.int32))
     send_halo(slice(3, 5))
+    lax.fori_loop(blocks - 2, blocks, own_block, 0)
 
     acc[...] = jnp.zeros_like(acc)
     width = 2 * LANES
@@ -533,8 +547,18 @@
 
     rim_places = (slice(planes, all_planes), halo_pieces, slice(0, ROWS), slice(ROWS, 2 * ROWS))
 
+    starts = list(range(0, inner, 8))
+
+    def edge_step():
+        if starts:
+            start = starts.pop(0)
+            add_edges(start)
+            contract(chunks - 1, start, 1)
+
     def rim_fields(first, stop):
         for f in range(first, stop):
+            if f % 2:
+                edge_step()
             for start in range(0, cells, width):
                 lanes = slice(start, start + width)
                 if 9 <= f < 15:
@@ -550,9 +574,8 @@
     form_flow(lambda c, lanes: halo_u[c, :, lanes], *rim_places)
     form_rates(lambda c, lanes: halo_s[c, :, lanes], *rim_places)
     rim_fields(0, FIELDS)
-    for start in range(0, inner, 8):
-        add_edges(start)
-        contract(chunks - 1, start, 1)
+    while starts:
+        edge_step()
     for chunk in range(chunks):
         for job in jobs(chunk, inner, planes):
             contract(*job)
@@ -674,7 +697,7 @@
             pltpu.SemaphoreType.DMA((12,)),
             pltpu.SemaphoreType.DMA((n_z,)),
             pltpu.SemaphoreType.DMA((n_z,)),
-            pltpu.SemaphoreType.DMA((8,)),
+            pltpu.SemaphoreType.DMA((10,)),
             pltpu.SemaphoreType.REGULAR((max((n_z // 2 - 1).bit_length(), 1),)),
             pltpu.SemaphoreType.REGULAR,
             pltpu.VMEM((planes, LANES), f32),

time: 17.7 us -> 17.7 us (level)
  no operation moved by 1% of the time
where the time goes in v7:
time: 17.7 us; the launch traced here: 17.5 us
  Pallas kernels  17 us (96%)
  local copies, waits for them, and re-layouts  0.51 us (3%)
    pallas_call x1, Pallas kernels, local(): pl.pallas_call(functools.partial(kernel, n_y, n_z), out_shape=jax.ShapeDt...  17 us
    unnamed x1, local copies, waits for them, and re-layouts  0.51 us

profile of v7, /device:TPU:0, one launch (start us, length us, event | category | flops | bytes accessed | tf_op | source)
XLA Modules:
  0.0 17.5 jit_solution(510060932475455049)
XLA Ops:
  0.0 17.0 %shard_map.46 = f32[1,96]{1,0:T(1,128)S(1)} custom-call(f32[3,96,768]{2,1,0:T(8,128)} %vel_hbm.1, bf16[6,96,768]{2,1,0:T(8,128)(2,1)} %strain_hbm.1, f32[1,96]{1,0:T(1,128)} %bitcast.3, s32[2,96]{1,0:T(2,128)} %reach_hbm.1), custom_call_target="tpu_custom_call" | custom-call | tf_op jit(solution)/shard_map/pallas_call | solution.py:663
  17.0 0.5 %copy.6 = f32[96]{0:T(128)} copy(f32[96]{0:T(128)S(1)} %bitcast.2) | data formatting | bytes 768
